TPU v7x, 512 devices: a whole 4x8x8 slice. The times are simulated.
512 devices in a mesh: row: 32 (over x, z), orb: 16 (over y, core).
Axes of the slice: x: 4, y: 8, z: 8, core: 2. Of those that a mesh axis runs over, the one named last changes fastest.
Arguments:
- orbitals: float32 [4096, 4096], P('row', 'orb'), may hold values from -700 to 700
Outputs:
- updated: float32 [4096, 4096], P('row', 'orb')
All inputs are finite; a program needn't handle non-finite values.
Results may differ from a plain program's by a relative error of at most 0.0065.
Values sent between devices are 32-bit elements; how exact they have to be, the bound alone decides.
No kernel may reach another device: no remote copies, remote signals or barrier semaphores. Data moves between devices by JAX's collectives and lax.ppermute only.
A program may use at most 64 MiB of HBM per device.

v0:
```python
import functools

import jax
import jax.numpy as jnp
from jax import lax
from jax.experimental import pallas as pl
from jax.experimental.pallas import tpu as pltpu
from jax.sharding import PartitionSpec as P


SUB = 8
LANE = 128
EXACT = lax.Precision.HIGHEST


def dot(left, right, left_dim=1, right_dim=0):
    dims = (((left_dim,), (right_dim,)), ((), ()))
    return lax.dot_general(
        left, right, dims, precision=EXACT, preferred_element_type=jnp.float32
    )


NEAR = 2


def factor(block):
    shape = (SUB, LANE)
    lane = lax.broadcasted_iota(jnp.int32, shape, 1)
    sub = lax.broadcasted_iota(jnp.int32, shape, 0)
    count = LANE // SUB
    tiles = [block[SUB * t : SUB * (t + 1), :] for t in range(count)]

    def full(vector):
        return jnp.broadcast_to(vector, shape)

    def pick(vector, i):
        return jnp.take_along_axis(vector, jnp.full(shape, i, jnp.int32), axis=0)

    for k in range(count):
        base = SUB * k
        inside = (lane >= base) & (lane < base + SUB)
        own = tiles[k]
        columns = [full(own[:, base + j : base + j + 1]) for j in range(SUB)]
        diag = [[pick(columns[j], i) for j in range(i + 1)] for i in range(SUB)]
        root, low = [], [[None] * SUB for _ in range(SUB)]
        for j in range(SUB):
            root.append(lax.rsqrt(diag[j][j]))
            for i in range(j + 1, SUB):
                low[i][j] = diag[i][j] * root[j]
            for i in range(j + 1, SUB):
                for m in range(j + 1, i + 1):
                    diag[i][m] = diag[i][m] - low[i][j] * low[m][j]

        def solve(vectors):
            for j in range(SUB):
                vectors[j] = vectors[j] * root[j]
                for i in range(j + 1, SUB):
                    vectors[i] = vectors[i] - low[i][j] * vectors[j]
            return vectors

        cleared = jnp.where(inside, jnp.where(lane - base == sub, 1.0, 0.0), own)
        done = solve([full(cleared[i : i + 1, :]) for i in range(SUB)])
        row = done[0]
        for i in range(1, SUB):
            row = jnp.where(sub == i, done[i], row)
        tiles[k] = row
        if k + 1 + NEAR < count:
            flipped = jnp.transpose(row)
        for t in range(k + 1, count):
            if t <= k + NEAR:
                left = solve([full(tiles[t][:, base + j : base + j + 1]) for j in range(SUB)])
            else:
                left = [full(flipped[SUB * t : SUB * (t + 1), j : j + 1]) for j in range(SUB)]
            terms = [left[j] * done[j] for j in range(SUB)]
            while len(terms) > 1:
                terms = [terms[i] + terms[i + 1] for i in range(0, len(terms), 2)]
            tiles[t] = jnp.where(inside, 0.0, tiles[t]) - terms[0]
    return jnp.concatenate(tiles, axis=0)


def span(i, size=LANE):
    return slice(size * i, size * (i + 1))


HALVES = (((0, 0), (0, 1), None, (1, 1), (0, 2), (0, 3)), ((2, 2), (2, 3), None, (3, 3), (1, 2), (1, 3)))
GRAM = 24
BASIS = 32


def call(kernel, outs, scalar, *args, scratch=()):
    return pl.pallas_call(
        kernel,
        out_shape=[jax.ShapeDtypeStruct(shape, jnp.float32) for shape in outs],
        in_specs=[pl.BlockSpec(memory_space=pltpu.SMEM)] + [pl.BlockSpec(memory_space=pltpu.VMEM)] * len(args),
        out_specs=[pl.BlockSpec(memory_space=pltpu.VMEM)] * len(outs),
        scratch_shapes=[pltpu.VMEM(shape, jnp.float32) for shape in scratch],
    )(scalar.reshape(1), *args)


def raw_blocks(core, mine_ref, other_ref):
    mine, other = mine_ref[...], other_ref[...]
    return jnp.where(core == 0, mine, other), jnp.where(core == 0, other, mine)


def inner_kernel(core_ref, mine_ref, other_ref, own_ref, out_ref, *, count):
    pieces = out_ref.shape[0]
    mine, other, own = mine_ref[...], other_ref[...], own_ref[...]
    first = core_ref[0] == 0
    for b, block in enumerate(raw_blocks(core_ref[0], mine_ref, other_ref)):
        gram = dot(block, own, 0, 0) / count
        for h in range(2):
            part = gram[:, span(h)].reshape(pieces // 2, BASIS // 2, LANE)
            out_ref[span(b, pieces // 2), span(h, BASIS // 2), :] = part
    square = dot(mine, mine, 0, 0) / count
    left = jnp.where(first, mine[:, :LANE], other[:, LANE:])
    cross = dot(left, jnp.where(first, other, mine), 0, 0) / count
    tiles = [square[span(i // 2), span(i % 2)] for i in range(4)] + [cross[:, span(i)] for i in range(2)]
    out_ref[:, BASIS:, :] = jnp.concatenate(tiles, axis=0).reshape(pieces, GRAM, LANE)


def total_kernel(core_ref, parts_ref, tiles_ref, out_ref):
    total = jnp.sum(parts_ref[...], axis=0)
    tiles_ref[...] = jnp.broadcast_to(total[None, BASIS:], tiles_ref.shape)
    out_ref[...] = jnp.broadcast_to(total[None, :BASIS], out_ref.shape)


def inverse_kernel(core_ref, mine_ref, other_ref, inv_ref, work_ref):
    n = inv_ref.shape[0]
    blocks = n // LANE
    first = core_ref[0] == 0
    work_ref[...] = jnp.zeros_like(work_ref)
    for half in range(2):
        for at, place in enumerate(HALVES[half]):
            if place is not None:
                mine, other = mine_ref[span(at), :], other_ref[span(at), :]
                tile = jnp.where(first == (half == 0), mine, other)
                work_ref[span(place[0]), span(place[1])] = tile
    for k in range(blocks):
        done = factor(work_ref[span(k), span(k)])
        row = lax.broadcasted_iota(jnp.int32, done.shape, 0)
        col = lax.broadcasted_iota(jnp.int32, done.shape, 1)
        done = jnp.where(row >= col, done, 0.0)
        work_ref[span(k), :] = dot(done, work_ref[span(k), :])
        work_ref[span(k), span(k)] = done
        for i in range(k + 1, blocks):
            up = work_ref[span(k), span(i)]
            work_ref[span(i), span(k)] = jnp.zeros((LANE, LANE), jnp.float32)
            work_ref[span(i), :] = work_ref[span(i), :] - dot(up, work_ref[span(k), :], 0, 0)
    for i in range(blocks):
        split = LANE * (i + 1)
        inv_ref[span(i), :split] = work_ref[span(i), :split]
        if split < n:
            inv_ref[span(i), split:] = jnp.zeros((LANE, n - split), jnp.float32)


def finish_kernel(index_ref, mine_ref, other_ref, inv_ref, gram_ref, own_ref, out_ref):
    width = own_ref.shape[1]
    pieces = gram_ref.shape[0]
    index = index_ref[0]
    zero, one = raw_blocks(index % 2, mine_ref, other_ref)

    def basis(b):
        left = dot(zero, inv_ref[span(b, width), :width], 1, 1)
        return left + dot(one, inv_ref[width:, width:], 1, 1) if b else left

    @pl.when(index == 0)
    def _():
        out_ref[...] = basis(0)

    @pl.when(index == 1)
    def _():
        out_ref[...] = basis(1)

    @pl.when(index > 1)
    def _():
        halves = [gram_ref[:, span(h, BASIS // 2), :].reshape(pieces * BASIS // 2, LANE) for h in range(2)]
        gram = jnp.concatenate(halves, axis=1)
        top = dot(inv_ref[:width, :width], gram[:width])
        low = dot(inv_ref[width:, :], gram)
        out_ref[...] = own_ref[...] - dot(basis(0), top) - dot(basis(1), low)


def swapped(pieces, axis):
    return lax.all_to_all(pieces, axis, 0, 0, tiled=True)


def steps(moves):
    return [(2 * source + c, 2 * target + c) for source, target in moves for c in range(2)]


def on_device(own):
    rows, width = own.shape
    many, groups = lax.axis_size("row"), lax.axis_size("orb")
    count = rows * many
    index = lax.axis_index("orb")
    core, chip = index % 2, index // 2
    pairs = [(i, i ^ 1) for i in range(groups)]

    first = lax.ppermute(own, "orb", steps([(0, 3)])) + lax.ppermute(own, "orb", steps([(0, 5)]))
    first = jnp.where(chip == 0, own, first)
    mine = first + lax.ppermute(first, "orb", steps([(0, 1), (3, 4), (5, 6)]))
    mine = mine + lax.ppermute(first, "orb", steps([(0, 7), (3, 2)]))
    other = lax.ppermute(mine, "orb", pairs)

    inner = call(functools.partial(inner_kernel, count=count), [(many, BASIS + GRAM, LANE)], core, mine, other, own)[0]
    tiles, gram = call(total_kernel, [(many, GRAM, LANE), (many, BASIS, LANE)], core, swapped(inner, "row"))
    tiles, gram = lax.optimization_barrier((swapped(tiles, "row").reshape(-1, LANE), gram))
    gram = swapped(gram, "row")
    others = lax.ppermute(tiles, "orb", pairs)
    inverse = call(
        inverse_kernel, [(2 * width, 2 * width)], core, tiles, others,
        scratch=[(2 * width, 2 * width)],
    )[0]
    return call(finish_kernel, [own.shape], index, mine, other, inverse, gram, own)[0]


def solution(mesh):
    return jax.shard_map(
        on_device,
        mesh=mesh,
        in_specs=(P("row", "orb"),),
        out_specs=P("row", "orb"),
        check_vma=False,
    )
```

profile of v0, /device:TPU:1, one launch (start us, length us, event | category | flops | bytes accessed | tf_op | source)
XLA Modules:
  0.0 120.2 jit_solution(15001795601176932903)
XLA Ops:
  0.0 7.5 %collective-permute-start.1 = (f32[128,256]{1,0:T(8,128)}, f32[128,256]{1,0:T(8,128)S(1)}, u32[]{:S(2)}, u32[]{:S(2)}) collective-permute-start(f32[128,256]{1,0:T(8,128)} %own_ref.3), channel_id=1, source_target_pairs={{0,10},{1,11},{16,26},{17,27},{32,42},{33,43},{48,58},{49,59},{64,... | collective-permute-start | bytes 393224 | tf_op jit(solution)/shard_map/ppermute | solution.py:199
  7.5 1.3 %collective-permute-start = (f32[128,256]{1,0:T(8,128)}, f32[128,256]{1,0:T(8,128)S(1)}, u32[]{:S(2)}, u32[]{:S(2)}) collective-permute-start(f32[128,256]{1,0:T(8,128)} %own_ref.3), channel_id=1, source_target_pairs={{0,6},{1,7},{16,22},{17,23},{32,38},{33,39},{48,54},{49,55},{64,70... | collective-permute-start | bytes 393224 | tf_op jit(solution)/shard_map/ppermute | solution.py:199
  8.8 1.1 collective-permute-done.1
  10.0 1.3 %collective-permute-done = f32[128,256]{1,0:T(8,128)S(1)} collective-permute-done((f32[128,256]{1,0:T(8,128)}, f32[128,256]{1,0:T(8,128)S(1)}, u32[]{:S(2)}, u32[]{:S(2)}) %collective-permute-start) | collective-permute-done | bytes 131104 | tf_op jit(solution)/shard_map/ppermute | solution.py:199
  11.3 0.9 add_select_fusion
  12.2 1.3 %collective-permute-start.3 = (f32[128,256]{1,0:T(8,128)S(1)}, f32[128,256]{1,0:T(8,128)S(1)}, u32[]{:S(2)}, u32[]{:S(2)}) collective-permute-start(f32[128,256]{1,0:T(8,128)S(1)} %add_select_fusion), channel_id=1, source_target_pairs={{0,14},{1,15},{6,4},{7,5},{16,30},{17,31},{22,20},{23,21},{32,46},... | collective-permute-start | bytes 393224 | tf_op jit(solution)/shard_map/ppermute | solution.py:202
  13.5 1.3 %collective-permute-start.2 = (f32[128,256]{1,0:T(8,128)S(1)}, f32[128,256]{1,0:T(8,128)S(1)}, u32[]{:S(2)}, u32[]{:S(2)}) collective-permute-start(f32[128,256]{1,0:T(8,128)S(1)} %add_select_fusion), channel_id=1, source_target_pairs={{0,2},{1,3},{6,8},{7,9},{10,12},{11,13},{16,18},{17,19},{22,24},{2... | collective-permute-start | bytes 393224 | tf_op jit(solution)/shard_map/ppermute | solution.py:201
  14.8 0.6 collective-permute-done.3
  15.4 1.3 %collective-permute-done.2 = f32[128,256]{1,0:T(8,128)S(1)} collective-permute-done((f32[128,256]{1,0:T(8,128)S(1)}, f32[128,256]{1,0:T(8,128)S(1)}, u32[]{:S(2)}, u32[]{:S(2)}) %collective-permute-start.2) | collective-permute-done | bytes 131104 | tf_op jit(solution)/shard_map/ppermute | solution.py:201
  16.8 0.0 copy-start.2
  16.8 4.0 %collective-permute-start.4 = (f32[128,256]{1,0:T(8,128)S(1)}, f32[128,256]{1,0:T(8,128)S(1)}, u32[]{:S(2)}, u32[]{:S(2)}) collective-permute-start(f32[128,256]{1,0:T(8,128)S(1)} %add_add_fusion.mine_ref), channel_id=1, source_target_pairs={{0,1},{1,0},{2,3},{3,2},{4,5},{5,4},{6,7},{7,6},{8,9},{9,8},{10,11... | collective-permute-start | bytes 393224 | tf_op jit(solution)/shard_map/ppermute | solution.py:203
  20.8 1.0 collective-permute-done.4.other_ref
  21.8 0.0 copy-start.3
  21.8 0.0 copy-done.2
  21.8 0.6 copy-done.3
  22.4 3.0 %shard_map.17 = f32[32,56,128]{2,1,0:T(8,128)} custom-call(s32[1]{0:T(128)} %bitcast.1.core_ref, f32[128,256]{1,0:T(8,128)} %copy-done.2, f32[128,256]{1,0:T(8,128)} %copy-done.3, f32[128,256]{1,0:T(8,128)} %own_ref.3), custom_call_target="tpu_custom_call" | custom-call | tf_op jit(solution)/shard_map/pallas_call | solution.py:91
  25.4 35.3 %all_to_all.15.parts_ref = f32[32,56,128]{2,1,0:T(8,128)} all-to-all(f32[32,56,128]{2,1,0:T(8,128)} %shard_map.17), channel_id=1, replica_groups=mesh['row'=32,'orb'=16] {'row'}, dimensions={0} | all-to-all | bytes 1835008 | tf_op jit(solution)/shard_map/all_to_all | solution.py:184
  60.7 2.2 %shard_map.18 = (f32[32,24,128]{2,1,0:T(8,128)}, f32[32,32,128]{2,1,0:T(8,128)}) custom-call(s32[1]{0:T(128)} %bitcast.1.core_ref, f32[32,56,128]{2,1,0:T(8,128)} %all_to_all.15.parts_ref), custom_call_target="tpu_custom_call" | custom-call | tf_op jit(solution)/shard_map/pallas_call | solution.py:91
  62.9 18.9 %all_to_all.16 = f32[32,24,128]{2,1,0:T(8,128)S(1)} all-to-all(f32[32,24,128]{2,1,0:T(8,128)} %get-tuple-element.9), channel_id=1, replica_groups=mesh['row'=32,'orb'=16] {'row'}, dimensions={0} | all-to-all | bytes 786432 | tf_op jit(solution)/shard_map/all_to_all | solution.py:184
  81.8 0.0 copy-start.1
  81.8 7.9 %all-to-all-start.2 = ((f32[32,32,128]{2,1,0:T(8,128)}), f32[32,32,128]{2,1,0:T(8,128)S(1)}, u32[]{:S(2)}, u32[]{:S(2)}) async-start(f32[32,32,128]{2,1,0:T(8,128)} %get-tuple-element.12), calls=%async_computation.2 | async-start | bytes 1048576 | tf_op jit(solution)/shard_map/all_to_all | solution.py:184
  89.7 0.0 copy-done.1
  89.7 4.0 %collective-permute-start.5 = (f32[768,128]{1,0:T(8,128)S(1)}, f32[768,128]{1,0:T(8,128)S(1)}, u32[]{:S(2)}, u32[]{:S(2)}) collective-permute-start(f32[768,128]{1,0:T(8,128)S(1)} %bitcast.3), channel_id=1, source_target_pairs={{0,1},{1,0},{2,3},{3,2},{4,5},{5,4},{6,7},{7,6},{8,9},{9,8},{10,11... | collective-permute-start | bytes 1179656 | tf_op jit(solution)/shard_map/ppermute | solution.py:209
  93.7 1.1 collective-permute-done.5.other_ref
  94.9 0.0 copy-start.4
  94.9 0.7 copy-done.4
  95.6 20.9 %shard_map.19.inv_ref = f32[512,512]{1,0:T(8,128)} custom-call(s32[1]{0:T(128)} %bitcast.1.core_ref, f32[768,128]{1,0:T(8,128)} %bitcast.4, f32[768,128]{1,0:T(8,128)} %copy-done.4), custom_call_target="tpu_custom_call" | custom-call | tf_op jit(solution)/shard_map/pallas_call | solution.py:91
  116.5 0.0 all-to-all-done.2.gram_ref
  116.5 0.0 copy-start
  116.5 0.8 copy-done
  117.3 2.8 %shard_map.20 = f32[128,256]{1,0:T(8,128)} custom-call(s32[1]{0:T(128)} %bitcast.index_ref, f32[128,256]{1,0:T(8,128)} %copy-done.2, f32[128,256]{1,0:T(8,128)} %copy-done.3, f32[512,512]{1,0:T(8,128)} %shard_map.19.inv_ref, f32[32,32,128]{2,1,0:T(8,128)} %copy-done, f32[128,256]{1,0:T(8,128)} %own_ref.3), custom_call_target="tpu_custom_call" | custom-call | tf_op jit(solution)/shard_map/pallas_call | solution.py:91
  (1 shorter events, 0.0 us)
Async XLA Ops:
  0.0 10.0 %collective-permute-start.1 = (f32[128,256]{1,0:T(8,128)}, f32[128,256]{1,0:T(8,128)S(1)}, u32[]{:S(2)}, u32[]{:S(2)}) collective-permute-start(f32[128,256]{1,0:T(8,128)} %own_ref.3), channel_id=1, source_target_pairs={{0,10},{1,11},{16,26},{17,27},{32,42},{33,43},{48,58},{49,59},{64,... | collective-permute-start | bytes 393224 | tf_op jit(solution)/shard_map/ppermute | solution.py:199
  7.5 3.8 %collective-permute-start = (f32[128,256]{1,0:T(8,128)}, f32[128,256]{1,0:T(8,128)S(1)}, u32[]{:S(2)}, u32[]{:S(2)}) collective-permute-start(f32[128,256]{1,0:T(8,128)} %own_ref.3), channel_id=1, source_target_pairs={{0,6},{1,7},{16,22},{17,23},{32,38},{33,39},{48,54},{49,55},{64,70... | collective-permute-start | bytes 393224 | tf_op jit(solution)/shard_map/ppermute | solution.py:199
  12.2 3.2 %collective-permute-start.3 = (f32[128,256]{1,0:T(8,128)S(1)}, f32[128,256]{1,0:T(8,128)S(1)}, u32[]{:S(2)}, u32[]{:S(2)}) collective-permute-start(f32[128,256]{1,0:T(8,128)S(1)} %add_select_fusion), channel_id=1, source_target_pairs={{0,14},{1,15},{6,4},{7,5},{16,30},{17,31},{22,20},{23,21},{32,46},... | collective-permute-start | bytes 393224 | tf_op jit(solution)/shard_map/ppermute | solution.py:202
  13.5 3.2 %collective-permute-start.2 = (f32[128,256]{1,0:T(8,128)S(1)}, f32[128,256]{1,0:T(8,128)S(1)}, u32[]{:S(2)}, u32[]{:S(2)}) collective-permute-start(f32[128,256]{1,0:T(8,128)S(1)} %add_select_fusion), channel_id=1, source_target_pairs={{0,2},{1,3},{6,8},{7,9},{10,12},{11,13},{16,18},{17,19},{22,24},{2... | collective-permute-start | bytes 393224 | tf_op jit(solution)/shard_map/ppermute | solution.py:201
  16.8 5.0 %copy-start.2 = (f32[128,256]{1,0:T(8,128)}, f32[128,256]{1,0:T(8,128)S(1)}, u32[]{:S(2)}) copy-start(f32[128,256]{1,0:T(8,128)S(1)} %add_add_fusion.mine_ref) | copy-start | bytes 393220
  16.8 5.0 %collective-permute-start.4 = (f32[128,256]{1,0:T(8,128)S(1)}, f32[128,256]{1,0:T(8,128)S(1)}, u32[]{:S(2)}, u32[]{:S(2)}) collective-permute-start(f32[128,256]{1,0:T(8,128)S(1)} %add_add_fusion.mine_ref), channel_id=1, source_target_pairs={{0,1},{1,0},{2,3},{3,2},{4,5},{5,4},{6,7},{7,6},{8,9},{9,8},{10,11... | collective-permute-start | bytes 393224 | tf_op jit(solution)/shard_map/ppermute | solution.py:203
  21.8 0.6 copy-start.3
  81.8 7.9 %copy-start.1 = (f32[32,24,128]{2,1,0:T(8,128)}, f32[32,24,128]{2,1,0:T(8,128)S(1)}, u32[]{:S(2)}) copy-start(f32[32,24,128]{2,1,0:T(8,128)S(1)} %all_to_all.16) | copy-start | bytes 1179652
  81.8 34.7 %all-to-all-start.2 = ((f32[32,32,128]{2,1,0:T(8,128)}), f32[32,32,128]{2,1,0:T(8,128)S(1)}, u32[]{:S(2)}, u32[]{:S(2)}) async-start(f32[32,32,128]{2,1,0:T(8,128)} %get-tuple-element.12), calls=%async_computation.2 | async-start | bytes 1048576 | tf_op jit(solution)/shard_map/all_to_all | solution.py:184
  89.7 5.2 %collective-permute-start.5 = (f32[768,128]{1,0:T(8,128)S(1)}, f32[768,128]{1,0:T(8,128)S(1)}, u32[]{:S(2)}, u32[]{:S(2)}) collective-permute-start(f32[768,128]{1,0:T(8,128)S(1)} %bitcast.3), channel_id=1, source_target_pairs={{0,1},{1,0},{2,3},{3,2},{4,5},{5,4},{6,7},{7,6},{8,9},{9,8},{10,11... | collective-permute-start | bytes 1179656 | tf_op jit(solution)/shard_map/ppermute | solution.py:209
  94.9 0.7 copy-start.4
  116.5 0.8 copy-start
where the time goes:
time: 123 us; the launch traced here: 120 us
  blocking collectives  54.2 us (44%)
  Pallas kernels  28.9 us (23%)
  starting transfers between devices  27.3 us (22%)
  waiting for transfers between devices  6.48 us (5%)
  local copies, waits for them, and re-layouts  2.22 us (2%)
    all_to_all x2, blocking collectives, swapped(): return lax.all_to_all(pieces, axis, 0, 0, tiled=True)  54.2 us
    pallas_call x4, Pallas kernels, call(): pl.pallas_call(kernel, out_shape=[jax.ShapeDtypeStruct(shape, jnp.float32...  28.9 us
    all_to_all x1, starting transfers between devices, swapped(): return lax.all_to_all(pieces, axis, 0, 0, tiled=True)  7.87 us
    ppermute x1, starting transfers between devices, on_device(): lax.ppermute(own, 'orb', steps([(0, 5)]))  7.48 us
    ppermute x1, starting transfers between devices, on_device(): others = lax.ppermute(tiles, 'orb', pairs)  4.03 us
    ppermute x1, starting transfers between devices, on_device(): other = lax.ppermute(mine, 'orb', pairs)  4.01 us
  transfers between devices with their start and end apart: 7, of which 6 were waited for; matrix products, arithmetic and copies ran while one was open for 0% of the time, Pallas kernels for 17%

commit v1 on v0

--- a/solution.py
+++ b/solution.py
@@ -64,17 +64,24 @@
         for i in range(1, SUB):
             row = jnp.where(sub == i, done[i], row)
         tiles[k] = row
-        if k + 1 + NEAR < count:
-            flipped = jnp.transpose(row)
-        for t in range(k + 1, count):
-            if t <= k + NEAR:
-                left = solve([full(tiles[t][:, base + j : base + j + 1]) for j in range(SUB)])
-            else:
-                left = [full(flipped[SUB * t : SUB * (t + 1), j : j + 1]) for j in range(SUB)]
+        near = range(k + 1, min(k + 1 + NEAR, count))
+        far = range(k + 1 + NEAR, count)
+        raws = [[full(tiles[t][:, base + j : base + j + 1]) for t in near] for j in range(SUB)]
+        for i, t in enumerate(near):
+            left = solve([raws[j][i] for j in range(SUB)])
             terms = [left[j] * done[j] for j in range(SUB)]
             while len(terms) > 1:
-                terms = [terms[i] + terms[i + 1] for i in range(0, len(terms), 2)]
+                terms = [terms[m] + terms[m + 1] for m in range(0, len(terms), 2)]
             tiles[t] = jnp.where(inside, 0.0, tiles[t]) - terms[0]
+        if far:
+            top = row.astype(jnp.bfloat16).astype(jnp.float32)
+            mid = (row - top).astype(jnp.bfloat16).astype(jnp.float32)
+            end = row - top - mid
+            left = jnp.concatenate([top, top, mid, mid, top, end], axis=0).astype(jnp.bfloat16)
+            right = jnp.concatenate([top, mid, top, mid, end, top], axis=0).astype(jnp.bfloat16)
+            terms = lax.dot_general(left, right, (((0,), (0,)), ((), ())), preferred_element_type=jnp.float32)
+            for t in far:
+                tiles[t] = jnp.where(inside, 0.0, tiles[t]) - terms[span(t, SUB), :]
     return jnp.concatenate(tiles, axis=0)
 
 
@@ -87,14 +94,15 @@
 BASIS = 32
 
 
-def call(kernel, outs, scalar, *args, scratch=()):
+def call(kernel, outs, scalar, *args, scratch=(), near=False):
+    kind = pltpu.VMEM if near else jax.ShapeDtypeStruct
     return pl.pallas_call(
         kernel,
-        out_shape=[jax.ShapeDtypeStruct(shape, jnp.float32) for shape in outs],
+        out_shape=[kind(shape, jnp.float32) for shape in outs],
         in_specs=[pl.BlockSpec(memory_space=pltpu.SMEM)] + [pl.BlockSpec(memory_space=pltpu.VMEM)] * len(args),
         out_specs=[pl.BlockSpec(memory_space=pltpu.VMEM)] * len(outs),
         scratch_shapes=[pltpu.VMEM(shape, jnp.float32) for shape in scratch],
-    )(scalar.reshape(1), *args)
+    )(scalar.reshape(1), *[pltpu.with_memory_space_constraint(a, pltpu.VMEM) for a in args])
 
 
 def raw_blocks(core, mine_ref, other_ref):
@@ -153,23 +161,26 @@
             inv_ref[span(i), split:] = jnp.zeros((LANE, n - split), jnp.float32)
 
 
-def finish_kernel(index_ref, mine_ref, other_ref, inv_ref, gram_ref, own_ref, out_ref):
+def basis_kernel(core_ref, mine_ref, other_ref, inv_ref, basis_ref):
+    zero, one = raw_blocks(core_ref[0], mine_ref, other_ref)
+    width = zero.shape[1]
+    basis_ref[:, :width] = dot(zero, inv_ref[:width, :width], 1, 1)
+    low = dot(zero, inv_ref[width:, :width], 1, 1)
+    basis_ref[:, width:] = low + dot(one, inv_ref[width:, width:], 1, 1)
+
+
+def finish_kernel(index_ref, basis_ref, inv_ref, gram_ref, own_ref, out_ref):
     width = own_ref.shape[1]
     pieces = gram_ref.shape[0]
     index = index_ref[0]
-    zero, one = raw_blocks(index % 2, mine_ref, other_ref)
-
-    def basis(b):
-        left = dot(zero, inv_ref[span(b, width), :width], 1, 1)
-        return left + dot(one, inv_ref[width:, width:], 1, 1) if b else left
 
     @pl.when(index == 0)
     def _():
-        out_ref[...] = basis(0)
+        out_ref[...] = basis_ref[:, :width]
 
     @pl.when(index == 1)
     def _():
-        out_ref[...] = basis(1)
+        out_ref[...] = basis_ref[:, width:]
 
     @pl.when(index > 1)
     def _():
@@ -177,7 +188,7 @@
         gram = jnp.concatenate(halves, axis=1)
         top = dot(inv_ref[:width, :width], gram[:width])
         low = dot(inv_ref[width:, :], gram)
-        out_ref[...] = own_ref[...] - dot(basis(0), top) - dot(basis(1), low)
+        out_ref[...] = own_ref[...] - dot(basis_ref[:, :width], top) - dot(basis_ref[:, width:], low)
 
 
 def swapped(pieces, axis):
@@ -209,9 +220,10 @@
     others = lax.ppermute(tiles, "orb", pairs)
     inverse = call(
         inverse_kernel, [(2 * width, 2 * width)], core, tiles, others,
-        scratch=[(2 * width, 2 * width)],
+        scratch=[(2 * width, 2 * width)], near=True,
     )[0]
-    return call(finish_kernel, [own.shape], index, mine, other, inverse, gram, own)[0]
+    basis = call(basis_kernel, [(rows, 2 * width)], core, mine, other, inverse, near=True)[0]
+    return call(finish_kernel, [own.shape], index, basis, inverse, gram, own)[0]
 
 
 def solution(mesh):

time: 123 us -> 110 us (0.89)
  the two profiles are of different devices: /device:TPU:1 before, /device:TPU:11 now
where the time goes in v1:
time: 110 us; the launch traced here: 109 us
  blocking collectives  53.6 us (49%)
  starting transfers between devices  20.4 us (19%)
  Pallas kernels  19.8 us (18%)
  waiting for transfers between devices  15.2 us (14%)
    all_to_all x2, blocking collectives, swapped(): return lax.all_to_all(pieces, axis, 0, 0, tiled=True)  53.6 us
    pallas_call x5, Pallas kernels, call(): pl.pallas_call(kernel, out_shape=[kind(shape, jnp.float32) for shape in o...  19.8 us
    ppermute x1, waiting for transfers between devices, on_device(): mine = first + lax.ppermute(first, 'orb', steps([(0, 1), (3, 4), (5, 6)]))  13.1 us
    all_to_all x1, starting transfers between devices, swapped(): return lax.all_to_all(pieces, axis, 0, 0, tiled=True)  8.38 us
    ppermute x1, starting transfers between devices, on_device(): other = lax.ppermute(mine, 'orb', pairs)  4.31 us
    ppermute x1, starting transfers between devices, on_device(): others = lax.ppermute(tiles, 'orb', pairs)  4.31 us
  transfers between devices with their start and end apart: 7, of which 3 were waited for; matrix products, arithmetic and copies ran while one was open for 0% of the time, Pallas kernels for 14%

profile of v1, /device:TPU:11, one launch (start us, length us, event | category | flops | bytes accessed | tf_op | source)
XLA Modules:
  0.0 109.2 jit_solution(14603870678717981589)
XLA Ops:
  0.0 0.7 collective-permute-start.1
  0.7 0.7 collective-permute-start
  1.4 0.0 collective-permute-done.1
  1.4 0.0 collective-permute-done
  1.4 0.0 copy-start
  1.4 0.8 collective-permute-start.3
  2.2 1.3 %collective-permute-start.2 = (f32[128,256]{1,0:T(8,128)S(1)}, f32[128,256]{1,0:T(8,128)S(1)}, u32[]{:S(2)}, u32[]{:S(2)}) collective-permute-start(f32[128,256]{1,0:T(8,128)S(1)} %add_select_fusion), channel_id=1, source_target_pairs={{0,2},{1,3},{6,8},{7,9},{10,12},{11,13},{16,18},{17,19},{22,24},{2... | collective-permute-start | bytes 393224 | tf_op jit(solution)/shard_map/ppermute | solution.py:212
  3.5 0.0 collective-permute-done.3
  3.6 13.1 %collective-permute-done.2 = f32[128,256]{1,0:T(8,128)S(1)} collective-permute-done((f32[128,256]{1,0:T(8,128)S(1)}, f32[128,256]{1,0:T(8,128)S(1)}, u32[]{:S(2)}, u32[]{:S(2)}) %collective-permute-start.2) | collective-permute-done | bytes 131104 | tf_op jit(solution)/shard_map/ppermute | solution.py:212
  16.7 4.3 %collective-permute-start.4 = (f32[128,256]{1,0:T(8,128)S(1)}, f32[128,256]{1,0:T(8,128)S(1)}, u32[]{:S(2)}, u32[]{:S(2)}) collective-permute-start(f32[128,256]{1,0:T(8,128)S(1)} %add_add_fusion.mine_ref), channel_id=1, source_target_pairs={{0,1},{1,0},{2,3},{3,2},{4,5},{5,4},{6,7},{7,6},{8,9},{9,8},{10,11... | collective-permute-start | bytes 393224 | tf_op jit(solution)/shard_map/ppermute | solution.py:214
  21.0 1.0 collective-permute-done.4.other_ref
  21.9 0.0 copy-done
  21.9 1.9 %shard_map.17 = f32[32,56,128]{2,1,0:T(8,128)} custom-call(s32[1]{0:T(128)} %bitcast.1.core_ref, f32[128,256]{1,0:T(8,128)S(1)} %add_add_fusion.mine_ref, f32[128,256]{1,0:T(8,128)S(1)} %collective-permute-done.4.other_ref, f32[128,256]{1,0:T(8,128)S(1)} %copy-done), custom_call_target="tpu_custom_call" | custom-call | tf_op jit(solution)/shard_map/pallas_call | solution.py:99
  23.8 33.7 %all_to_all.15.parts_ref = f32[32,56,128]{2,1,0:T(8,128)S(1)} all-to-all(f32[32,56,128]{2,1,0:T(8,128)} %shard_map.17), channel_id=1, replica_groups=mesh['row'=32,'orb'=16] {'row'}, dimensions={0} | all-to-all | bytes 1835008 | tf_op jit(solution)/shard_map/all_to_all | solution.py:195
  57.5 1.0 shard_map.18
  58.5 19.9 %all_to_all.16 = f32[32,24,128]{2,1,0:T(8,128)S(1)} all-to-all(f32[32,24,128]{2,1,0:T(8,128)} %get-tuple-element.9), channel_id=1, replica_groups=mesh['row'=32,'orb'=16] {'row'}, dimensions={0} | all-to-all | bytes 786432 | tf_op jit(solution)/shard_map/all_to_all | solution.py:195
  78.4 8.4 %all-to-all-start.2 = ((f32[32,32,128]{2,1,0:T(8,128)}), f32[32,32,128]{2,1,0:T(8,128)S(1)}, u32[]{:S(2)}, u32[]{:S(2)}) async-start(f32[32,32,128]{2,1,0:T(8,128)} %get-tuple-element.12), calls=%async_computation.2 | async-start | bytes 1048576 | tf_op jit(solution)/shard_map/all_to_all | solution.py:195
  86.8 4.3 %collective-permute-start.5 = (f32[768,128]{1,0:T(8,128)S(1)}, f32[768,128]{1,0:T(8,128)S(1)}, u32[]{:S(2)}, u32[]{:S(2)}) collective-permute-start(f32[768,128]{1,0:T(8,128)S(1)} %bitcast.3), channel_id=1, source_target_pairs={{0,1},{1,0},{2,3},{3,2},{4,5},{5,4},{6,7},{7,6},{8,9},{9,8},{10,11... | collective-permute-start | bytes 1179656 | tf_op jit(solution)/shard_map/ppermute | solution.py:220
  91.1 1.1 %collective-permute-done.5.other_ref = f32[768,128]{1,0:T(8,128)S(1)} collective-permute-done((f32[768,128]{1,0:T(8,128)S(1)}, f32[768,128]{1,0:T(8,128)S(1)}, u32[]{:S(2)}, u32[]{:S(2)}) %collective-permute-start.5) | collective-permute-done | bytes 393248 | tf_op jit(solution)/shard_map/ppermute | solution.py:220
  92.3 14.0 %shard_map.19.inv_ref = f32[512,512]{1,0:T(8,128)S(1)} custom-call(s32[1]{0:T(128)} %bitcast.1.core_ref, f32[768,128]{1,0:T(8,128)S(1)} %bitcast.4, f32[768,128]{1,0:T(8,128)S(1)} %collective-permute-done.5.other_ref), custom_call_target="tpu_custom_call" | custom-call | tf_op jit(solution)/shard_map/pallas_call | solution.py:99
  106.3 0.9 shard_map.20.basis_ref
  107.2 0.0 all-to-all-done.2.gram_ref
  107.2 2.0 %shard_map.21 = f32[128,256]{1,0:T(8,128)} custom-call(s32[1]{0:T(128)} %bitcast.index_ref, f32[128,512]{1,0:T(8,128)S(1)} %shard_map.20.basis_ref, f32[512,512]{1,0:T(8,128)S(1)} %shard_map.19.inv_ref, f32[32,32,128]{2,1,0:T(8,128)S(1)} %all-to-all-done.2.gram_ref, f32[128,256]{1,0:T(8,128)S(1)} %copy-done), custom_call_target="tpu_custom_call" | custom-call | tf_op jit(solution)/shard_map/pallas_call | solution.py:99
  (2 shorter events, 0.1 us)
Async XLA Ops:
  0.0 1.4 %collective-permute-start.1 = (f32[128,256]{1,0:T(8,128)}, f32[128,256]{1,0:T(8,128)S(1)}, u32[]{:S(2)}, u32[]{:S(2)}) collective-permute-start(f32[128,256]{1,0:T(8,128)} %own_ref.3), channel_id=1, source_target_pairs={{0,10},{1,11},{16,26},{17,27},{32,42},{33,43},{48,58},{49,59},{64,... | collective-permute-start | bytes 393224 | tf_op jit(solution)/shard_map/ppermute | solution.py:210
  0.7 0.7 collective-permute-start
  1.4 20.5 %copy-start = (f32[128,256]{1,0:T(8,128)S(1)}, f32[128,256]{1,0:T(8,128)}, u32[]{:S(2)}) copy-start(f32[128,256]{1,0:T(8,128)} %own_ref.3) | copy-start | bytes 393220
  1.4 2.1 %collective-permute-start.3 = (f32[128,256]{1,0:T(8,128)S(1)}, f32[128,256]{1,0:T(8,128)S(1)}, u32[]{:S(2)}, u32[]{:S(2)}) collective-permute-start(f32[128,256]{1,0:T(8,128)S(1)} %add_select_fusion), channel_id=1, source_target_pairs={{0,14},{1,15},{6,4},{7,5},{16,30},{17,31},{22,20},{23,21},{32,46},... | collective-permute-start | bytes 393224 | tf_op jit(solution)/shard_map/ppermute | solution.py:213
  2.2 14.4 %collective-permute-start.2 = (f32[128,256]{1,0:T(8,128)S(1)}, f32[128,256]{1,0:T(8,128)S(1)}, u32[]{:S(2)}, u32[]{:S(2)}) collective-permute-start(f32[128,256]{1,0:T(8,128)S(1)} %add_select_fusion), channel_id=1, source_target_pairs={{0,2},{1,3},{6,8},{7,9},{10,12},{11,13},{16,18},{17,19},{22,24},{2... | collective-permute-start | bytes 393224 | tf_op jit(solution)/shard_map/ppermute | solution.py:212
  16.7 5.3 %collective-permute-start.4 = (f32[128,256]{1,0:T(8,128)S(1)}, f32[128,256]{1,0:T(8,128)S(1)}, u32[]{:S(2)}, u32[]{:S(2)}) collective-permute-start(f32[128,256]{1,0:T(8,128)S(1)} %add_add_fusion.mine_ref), channel_id=1, source_target_pairs={{0,1},{1,0},{2,3},{3,2},{4,5},{5,4},{6,7},{7,6},{8,9},{9,8},{10,11... | collective-permute-start | bytes 393224 | tf_op jit(solution)/shard_map/ppermute | solution.py:214
  78.4 28.8 %all-to-all-start.2 = ((f32[32,32,128]{2,1,0:T(8,128)}), f32[32,32,128]{2,1,0:T(8,128)S(1)}, u32[]{:S(2)}, u32[]{:S(2)}) async-start(f32[32,32,128]{2,1,0:T(8,128)} %get-tuple-element.12), calls=%async_computation.2 | async-start | bytes 1048576 | tf_op jit(solution)/shard_map/all_to_all | solution.py:195
  86.8 5.5 %collective-permute-start.5 = (f32[768,128]{1,0:T(8,128)S(1)}, f32[768,128]{1,0:T(8,128)S(1)}, u32[]{:S(2)}, u32[]{:S(2)}) collective-permute-start(f32[768,128]{1,0:T(8,128)S(1)} %bitcast.3), channel_id=1, source_target_pairs={{0,1},{1,0},{2,3},{3,2},{4,5},{5,4},{6,7},{7,6},{8,9},{9,8},{10,11... | collective-permute-start | bytes 1179656 | tf_op jit(solution)/shard_map/ppermute | solution.py:220

commit v2 on v1

--- a/solution.py
+++ b/solution.py
@@ -94,11 +94,11 @@
 BASIS = 32
 
 
-def call(kernel, outs, scalar, *args, scratch=(), near=False):
-    kind = pltpu.VMEM if near else jax.ShapeDtypeStruct
+def call(kernel, outs, scalar, *args, scratch=(), near=(True,)):
+    kinds = [pltpu.VMEM if here else jax.ShapeDtypeStruct for here in near]
     return pl.pallas_call(
         kernel,
-        out_shape=[kind(shape, jnp.float32) for shape in outs],
+        out_shape=[kind(shape, jnp.float32) for kind, shape in zip(kinds, outs)],
         in_specs=[pl.BlockSpec(memory_space=pltpu.SMEM)] + [pl.BlockSpec(memory_space=pltpu.VMEM)] * len(args),
         out_specs=[pl.BlockSpec(memory_space=pltpu.VMEM)] * len(outs),
         scratch_shapes=[pltpu.VMEM(shape, jnp.float32) for shape in scratch],
@@ -148,12 +148,16 @@
         row = lax.broadcasted_iota(jnp.int32, done.shape, 0)
         col = lax.broadcasted_iota(jnp.int32, done.shape, 1)
         done = jnp.where(row >= col, done, 0.0)
-        work_ref[span(k), :] = dot(done, work_ref[span(k), :])
+        sides = [slice(0, LANE * k), slice(LANE * (k + 1), n)]
+        for side in sides:
+            if side.start < side.stop:
+                work_ref[span(k), side] = dot(done, work_ref[span(k), side])
         work_ref[span(k), span(k)] = done
         for i in range(k + 1, blocks):
             up = work_ref[span(k), span(i)]
             work_ref[span(i), span(k)] = jnp.zeros((LANE, LANE), jnp.float32)
-            work_ref[span(i), :] = work_ref[span(i), :] - dot(up, work_ref[span(k), :], 0, 0)
+            for side in (slice(LANE * i, n), slice(0, LANE * (k + 1))):
+                work_ref[span(i), side] = work_ref[span(i), side] - dot(up, work_ref[span(k), side], 0, 0)
     for i in range(blocks):
         split = LANE * (i + 1)
         inv_ref[span(i), :split] = work_ref[span(i), :split]
@@ -161,34 +165,33 @@
             inv_ref[span(i), split:] = jnp.zeros((LANE, n - split), jnp.float32)
 
 
-def basis_kernel(core_ref, mine_ref, other_ref, inv_ref, basis_ref):
-    zero, one = raw_blocks(core_ref[0], mine_ref, other_ref)
+def basis_kernel(index_ref, mine_ref, other_ref, inv_ref, basis_ref):
+    zero, one = raw_blocks(index_ref[0] % 2, mine_ref, other_ref)
     width = zero.shape[1]
-    basis_ref[:, :width] = dot(zero, inv_ref[:width, :width], 1, 1)
-    low = dot(zero, inv_ref[width:, :width], 1, 1)
-    basis_ref[:, width:] = low + dot(one, inv_ref[width:, width:], 1, 1)
-
-
-def finish_kernel(index_ref, basis_ref, inv_ref, gram_ref, own_ref, out_ref):
+    top = dot(zero, inv_ref[:width, :width], 1, 1)
+    low = dot(zero, inv_ref[width:, :width], 1, 1) + dot(one, inv_ref[width:, width:], 1, 1)
+    basis_ref[:, :width] = jnp.where(index_ref[0] == 1, low, top)
+    basis_ref[:, width:] = low
+
+    @pl.when(index_ref[0] > 1)
+    def _():
+        basis_ref[:, :width] = dot(top, inv_ref[:width, :width]) + dot(low, inv_ref[width:, :width])
+        basis_ref[:, width:] = dot(low, inv_ref[width:, width:])
+
+
+def finish_kernel(index_ref, basis_ref, gram_ref, own_ref, out_ref):
     width = own_ref.shape[1]
     pieces = gram_ref.shape[0]
-    index = index_ref[0]
-
-    @pl.when(index == 0)
+
+    @pl.when(index_ref[0] < 2)
     def _():
         out_ref[...] = basis_ref[:, :width]
 
-    @pl.when(index == 1)
+    @pl.when(index_ref[0] > 1)
     def _():
-        out_ref[...] = basis_ref[:, width:]
-
-    @pl.when(index > 1)
-    def _():
-        halves = [gram_ref[:, span(h, BASIS // 2), :].reshape(pieces * BASIS // 2, LANE) for h in range(2)]
-        gram = jnp.concatenate(halves, axis=1)
-        top = dot(inv_ref[:width, :width], gram[:width])
-        low = dot(inv_ref[width:, :], gram)
-        out_ref[...] = own_ref[...] - dot(basis_ref[:, :width], top) - dot(basis_ref[:, width:], low)
+        for h in range(2):
+            gram = gram_ref[:, span(h, BASIS // 2), :].reshape(pieces * BASIS // 2, LANE)
+            out_ref[:, span(h)] = own_ref[:, span(h)] - dot(basis_ref[...], gram)
 
 
 def swapped(pieces, axis):
@@ -214,16 +217,19 @@
     other = lax.ppermute(mine, "orb", pairs)
 
     inner = call(functools.partial(inner_kernel, count=count), [(many, BASIS + GRAM, LANE)], core, mine, other, own)[0]
-    tiles, gram = call(total_kernel, [(many, GRAM, LANE), (many, BASIS, LANE)], core, swapped(inner, "row"))
+    tiles, gram = call(
+        total_kernel, [(many, GRAM, LANE), (many, BASIS, LANE)], core, swapped(inner, "row"),
+        near=(True, False),
+    )
     tiles, gram = lax.optimization_barrier((swapped(tiles, "row").reshape(-1, LANE), gram))
     gram = swapped(gram, "row")
     others = lax.ppermute(tiles, "orb", pairs)
     inverse = call(
         inverse_kernel, [(2 * width, 2 * width)], core, tiles, others,
-        scratch=[(2 * width, 2 * width)], near=True,
+        scratch=[(2 * width, 2 * width)],
     )[0]
-    basis = call(basis_kernel, [(rows, 2 * width)], core, mine, other, inverse, near=True)[0]
-    return call(finish_kernel, [own.shape], index, basis, inverse, gram, own)[0]
+    basis = call(basis_kernel, [(rows, 2 * width)], index, mine, other, inverse)[0]
+    return call(finish_kernel, [own.shape], index, basis, gram, own, near=(False,))[0]
 
 
 def solution(mesh):

time: 110 us -> 108 us (0.982)
  the two profiles are of different devices: /device:TPU:11 before, /device:TPU:1 now
where the time goes in v2:
time: 108 us; the launch traced here: 106 us
  blocking collectives  53.7 us (50%)
  starting transfers between devices  27.4 us (25%)
  Pallas kernels  17.1 us (16%)
  waiting for transfers between devices  6.48 us (6%)
    all_to_all x2, blocking collectives, swapped(): return lax.all_to_all(pieces, axis, 0, 0, tiled=True)  53.7 us
    pallas_call x5, Pallas kernels, call(): pl.pallas_call(kernel, out_shape=[kind(shape, jnp.float32) for kind, shap...  17.1 us
    all_to_all x1, starting transfers between devices, swapped(): return lax.all_to_all(pieces, axis, 0, 0, tiled=True)  7.87 us
    ppermute x1, starting transfers between devices, on_device(): lax.ppermute(own, 'orb', steps([(0, 5)]))  7.48 us
    ppermute x1, starting transfers between devices, on_device(): others = lax.ppermute(tiles, 'orb', pairs)  4.03 us
    ppermute x1, starting transfers between devices, on_device(): other = lax.ppermute(mine, 'orb', pairs)  4.01 us
  transfers between devices with their start and end apart: 7, of which 6 were waited for; matrix products, arithmetic and copies ran while one was open for 0% of the time, Pallas kernels for 14%

profile of v2, /device:TPU:1, one launch (start us, length us, event | category | flops | bytes accessed | tf_op | source)
XLA Modules:
  0.0 105.8 jit_solution(2068691143604333184)
XLA Ops:
  0.0 7.5 %collective-permute-start.1 = (f32[128,256]{1,0:T(8,128)}, f32[128,256]{1,0:T(8,128)S(1)}, u32[]{:S(2)}, u32[]{:S(2)}) collective-permute-start(f32[128,256]{1,0:T(8,128)} %own_ref.3), channel_id=1, source_target_pairs={{0,10},{1,11},{16,26},{17,27},{32,42},{33,43},{48,58},{49,59},{64,... | collective-permute-start | bytes 393224 | tf_op jit(solution)/shard_map/ppermute | solution.py:213
  7.5 1.3 %collective-permute-start = (f32[128,256]{1,0:T(8,128)}, f32[128,256]{1,0:T(8,128)S(1)}, u32[]{:S(2)}, u32[]{:S(2)}) collective-permute-start(f32[128,256]{1,0:T(8,128)} %own_ref.3), channel_id=1, source_target_pairs={{0,6},{1,7},{16,22},{17,23},{32,38},{33,39},{48,54},{49,55},{64,70... | collective-permute-start | bytes 393224 | tf_op jit(solution)/shard_map/ppermute | solution.py:213
  8.8 1.1 %collective-permute-done.1 = f32[128,256]{1,0:T(8,128)S(1)} collective-permute-done((f32[128,256]{1,0:T(8,128)}, f32[128,256]{1,0:T(8,128)S(1)}, u32[]{:S(2)}, u32[]{:S(2)}) %collective-permute-start.1) | collective-permute-done | bytes 131104 | tf_op jit(solution)/shard_map/ppermute | solution.py:213
  10.0 1.3 %collective-permute-done = f32[128,256]{1,0:T(8,128)S(1)} collective-permute-done((f32[128,256]{1,0:T(8,128)}, f32[128,256]{1,0:T(8,128)S(1)}, u32[]{:S(2)}, u32[]{:S(2)}) %collective-permute-start) | collective-permute-done | bytes 131104 | tf_op jit(solution)/shard_map/ppermute | solution.py:213
  11.3 0.9 add_select_fusion
  12.2 0.0 copy-start
  12.2 1.4 %collective-permute-start.3 = (f32[128,256]{1,0:T(8,128)S(1)}, f32[128,256]{1,0:T(8,128)S(1)}, u32[]{:S(2)}, u32[]{:S(2)}) collective-permute-start(f32[128,256]{1,0:T(8,128)S(1)} %add_select_fusion), channel_id=1, source_target_pairs={{0,14},{1,15},{6,4},{7,5},{16,30},{17,31},{22,20},{23,21},{32,46},... | collective-permute-start | bytes 393224 | tf_op jit(solution)/shard_map/ppermute | solution.py:216
  13.6 1.3 %collective-permute-start.2 = (f32[128,256]{1,0:T(8,128)S(1)}, f32[128,256]{1,0:T(8,128)S(1)}, u32[]{:S(2)}, u32[]{:S(2)}) collective-permute-start(f32[128,256]{1,0:T(8,128)S(1)} %add_select_fusion), channel_id=1, source_target_pairs={{0,2},{1,3},{6,8},{7,9},{10,12},{11,13},{16,18},{17,19},{22,24},{2... | collective-permute-start | bytes 393224 | tf_op jit(solution)/shard_map/ppermute | solution.py:215
  15.0 0.6 collective-permute-done.3
  15.6 1.3 %collective-permute-done.2 = f32[128,256]{1,0:T(8,128)S(1)} collective-permute-done((f32[128,256]{1,0:T(8,128)S(1)}, f32[128,256]{1,0:T(8,128)S(1)}, u32[]{:S(2)}, u32[]{:S(2)}) %collective-permute-start.2) | collective-permute-done | bytes 131104 | tf_op jit(solution)/shard_map/ppermute | solution.py:215
  16.9 4.0 %collective-permute-start.4 = (f32[128,256]{1,0:T(8,128)S(1)}, f32[128,256]{1,0:T(8,128)S(1)}, u32[]{:S(2)}, u32[]{:S(2)}) collective-permute-start(f32[128,256]{1,0:T(8,128)S(1)} %add_add_fusion.mine_ref), channel_id=1, source_target_pairs={{0,1},{1,0},{2,3},{3,2},{4,5},{5,4},{6,7},{7,6},{8,9},{9,8},{10,11... | collective-permute-start | bytes 393224 | tf_op jit(solution)/shard_map/ppermute | solution.py:217
  20.9 1.0 collective-permute-done.4.other_ref
  21.9 0.0 copy-done
  21.9 0.9 shard_map.17
  22.8 35.0 %all_to_all.15.parts_ref = f32[32,56,128]{2,1,0:T(8,128)S(1)} all-to-all(f32[32,56,128]{2,1,0:T(8,128)S(1)} %shard_map.17), channel_id=1, replica_groups=mesh['row'=32,'orb'=16] {'row'}, dimensions={0} | all-to-all | bytes 1835008 | tf_op jit(solution)/shard_map/all_to_all | solution.py:198
  57.8 0.9 shard_map.18
  58.7 18.7 %all_to_all.16 = f32[32,24,128]{2,1,0:T(8,128)S(1)} all-to-all(f32[32,24,128]{2,1,0:T(8,128)S(1)} %get-tuple-element.9), channel_id=1, replica_groups=mesh['row'=32,'orb'=16] {'row'}, dimensions={0} | all-to-all | bytes 786432 | tf_op jit(solution)/shard_map/all_to_all | solution.py:198
  77.4 7.9 %all-to-all-start.2 = ((f32[32,32,128]{2,1,0:T(8,128)}), f32[32,32,128]{2,1,0:T(8,128)S(1)}, u32[]{:S(2)}, u32[]{:S(2)}) async-start(f32[32,32,128]{2,1,0:T(8,128)} %get-tuple-element.12), calls=%async_computation.2 | async-start | bytes 1048576 | tf_op jit(solution)/shard_map/all_to_all | solution.py:198
  85.3 4.0 %collective-permute-start.5 = (f32[768,128]{1,0:T(8,128)S(1)}, f32[768,128]{1,0:T(8,128)S(1)}, u32[]{:S(2)}, u32[]{:S(2)}) collective-permute-start(f32[768,128]{1,0:T(8,128)S(1)} %bitcast.3), channel_id=1, source_target_pairs={{0,1},{1,0},{2,3},{3,2},{4,5},{5,4},{6,7},{7,6},{8,9},{9,8},{10,11... | collective-permute-start | bytes 1179656 | tf_op jit(solution)/shard_map/ppermute | solution.py:226
  89.4 1.1 %collective-permute-done.5.other_ref = f32[768,128]{1,0:T(8,128)S(1)} collective-permute-done((f32[768,128]{1,0:T(8,128)S(1)}, f32[768,128]{1,0:T(8,128)S(1)}, u32[]{:S(2)}, u32[]{:S(2)}) %collective-permute-start.5) | collective-permute-done | bytes 393248 | tf_op jit(solution)/shard_map/ppermute | solution.py:226
  90.5 13.7 %shard_map.19.inv_ref = f32[512,512]{1,0:T(8,128)S(1)} custom-call(s32[1]{0:T(128)} %bitcast.1.core_ref, f32[768,128]{1,0:T(8,128)S(1)} %bitcast.4, f32[768,128]{1,0:T(8,128)S(1)} %collective-permute-done.5.other_ref), custom_call_target="tpu_custom_call" | custom-call | tf_op jit(solution)/shard_map/pallas_call | solution.py:99
  104.2 0.9 shard_map.20.basis_ref
  105.1 0.0 all-to-all-done.2.gram_ref
  105.2 0.7 shard_map.21
  (1 shorter events, 0.0 us)
Async XLA Ops:
  0.0 10.0 %collective-permute-start.1 = (f32[128,256]{1,0:T(8,128)}, f32[128,256]{1,0:T(8,128)S(1)}, u32[]{:S(2)}, u32[]{:S(2)}) collective-permute-start(f32[128,256]{1,0:T(8,128)} %own_ref.3), channel_id=1, source_target_pairs={{0,10},{1,11},{16,26},{17,27},{32,42},{33,43},{48,58},{49,59},{64,... | collective-permute-start | bytes 393224 | tf_op jit(solution)/shard_map/ppermute | solution.py:213
  7.5 3.8 %collective-permute-start = (f32[128,256]{1,0:T(8,128)}, f32[128,256]{1,0:T(8,128)S(1)}, u32[]{:S(2)}, u32[]{:S(2)}) collective-permute-start(f32[128,256]{1,0:T(8,128)} %own_ref.3), channel_id=1, source_target_pairs={{0,6},{1,7},{16,22},{17,23},{32,38},{33,39},{48,54},{49,55},{64,70... | collective-permute-start | bytes 393224 | tf_op jit(solution)/shard_map/ppermute | solution.py:213
  12.2 9.7 %copy-start = (f32[128,256]{1,0:T(8,128)S(1)}, f32[128,256]{1,0:T(8,128)}, u32[]{:S(2)}) copy-start(f32[128,256]{1,0:T(8,128)} %own_ref.3) | copy-start | bytes 393220
  12.2 3.4 %collective-permute-start.3 = (f32[128,256]{1,0:T(8,128)S(1)}, f32[128,256]{1,0:T(8,128)S(1)}, u32[]{:S(2)}, u32[]{:S(2)}) collective-permute-start(f32[128,256]{1,0:T(8,128)S(1)} %add_select_fusion), channel_id=1, source_target_pairs={{0,14},{1,15},{6,4},{7,5},{16,30},{17,31},{22,20},{23,21},{32,46},... | collective-permute-start | bytes 393224 | tf_op jit(solution)/shard_map/ppermute | solution.py:216
  13.6 3.2 %collective-permute-start.2 = (f32[128,256]{1,0:T(8,128)S(1)}, f32[128,256]{1,0:T(8,128)S(1)}, u32[]{:S(2)}, u32[]{:S(2)}) collective-permute-start(f32[128,256]{1,0:T(8,128)S(1)} %add_select_fusion), channel_id=1, source_target_pairs={{0,2},{1,3},{6,8},{7,9},{10,12},{11,13},{16,18},{17,19},{22,24},{2... | collective-permute-start | bytes 393224 | tf_op jit(solution)/shard_map/ppermute | solution.py:215
  16.9 5.0 %collective-permute-start.4 = (f32[128,256]{1,0:T(8,128)S(1)}, f32[128,256]{1,0:T(8,128)S(1)}, u32[]{:S(2)}, u32[]{:S(2)}) collective-permute-start(f32[128,256]{1,0:T(8,128)S(1)} %add_add_fusion.mine_ref), channel_id=1, source_target_pairs={{0,1},{1,0},{2,3},{3,2},{4,5},{5,4},{6,7},{7,6},{8,9},{9,8},{10,11... | collective-permute-start | bytes 393224 | tf_op jit(solution)/shard_map/ppermute | solution.py:217
  77.4 27.7 %all-to-all-start.2 = ((f32[32,32,128]{2,1,0:T(8,128)}), f32[32,32,128]{2,1,0:T(8,128)S(1)}, u32[]{:S(2)}, u32[]{:S(2)}) async-start(f32[32,32,128]{2,1,0:T(8,128)} %get-tuple-element.12), calls=%async_computation.2 | async-start | bytes 1048576 | tf_op jit(solution)/shard_map/all_to_all | solution.py:198
  85.3 5.2 %collective-permute-start.5 = (f32[768,128]{1,0:T(8,128)S(1)}, f32[768,128]{1,0:T(8,128)S(1)}, u32[]{:S(2)}, u32[]{:S(2)}) collective-permute-start(f32[768,128]{1,0:T(8,128)S(1)} %bitcast.3), channel_id=1, source_target_pairs={{0,1},{1,0},{2,3},{3,2},{4,5},{5,4},{6,7},{7,6},{8,9},{9,8},{10,11... | collective-permute-start | bytes 1179656 | tf_op jit(solution)/shard_map/ppermute | solution.py:226

commit v3 on v2

--- a/solution.py
+++ b/solution.py
@@ -89,8 +89,8 @@
     return slice(size * i, size * (i + 1))
 
 
-HALVES = (((0, 0), (0, 1), None, (1, 1), (0, 2), (0, 3)), ((2, 2), (2, 3), None, (3, 3), (1, 2), (1, 3)))
-GRAM = 24
+HALVES = (((0, 0), (1, 1), (0, 1), (0, 2), (0, 3)), ((2, 2), (3, 3), (2, 3), (1, 2), (1, 3)))
+GRAM = 17
 BASIS = 32
 
 
@@ -110,39 +110,72 @@
     return jnp.where(core == 0, mine, other), jnp.where(core == 0, other, mine)
 
 
-def inner_kernel(core_ref, mine_ref, other_ref, own_ref, out_ref, *, count):
-    pieces = out_ref.shape[0]
+def on_diagonal():
+    row = lax.broadcasted_iota(jnp.int32, (LANE, LANE), 0)
+    col = lax.broadcasted_iota(jnp.int32, (LANE, LANE), 1)
+    return row, col
+
+
+def inner_kernel(core_ref, mine_ref, other_ref, own_ref, out_ref, *, count, pieces):
     mine, other, own = mine_ref[...], other_ref[...], own_ref[...]
     first = core_ref[0] == 0
+    size, half = BASIS + GRAM, BASIS // 2
     for b, block in enumerate(raw_blocks(core_ref[0], mine_ref, other_ref)):
         gram = dot(block, own, 0, 0) / count
-        for h in range(2):
-            part = gram[:, span(h)].reshape(pieces // 2, BASIS // 2, LANE)
-            out_ref[span(b, pieces // 2), span(h, BASIS // 2), :] = part
+        for p in range(pieces // 2):
+            at = size * (b * (pieces // 2) + p)
+            for h in range(2):
+                out_ref[at + half * h : at + half * (h + 1), :] = gram[span(p, half), span(h)]
     square = dot(mine, mine, 0, 0) / count
     left = jnp.where(first, mine[:, :LANE], other[:, LANE:])
     cross = dot(left, jnp.where(first, other, mine), 0, 0) / count
-    tiles = [square[span(i // 2), span(i % 2)] for i in range(4)] + [cross[:, span(i)] for i in range(2)]
-    out_ref[:, BASIS:, :] = jnp.concatenate(tiles, axis=0).reshape(pieces, GRAM, LANE)
+    row, col = on_diagonal()
+    second = square[span(1), span(1)]
+    folded = jnp.where(row <= col, square[span(0), span(0)], second)
+    diagonal = jnp.sum(jnp.where(row == col, second, 0.0), axis=0, keepdims=True)
+    tiles = [folded, square[span(0), span(1)], cross[:, span(0)], cross[:, span(1)]]
+    each = GRAM - 1
+    for p in range(pieces):
+        at = size * p + BASIS
+        tile, line = divmod(p * each, LANE)
+        out_ref[at : at + each, :] = tiles[tile][line : line + each, :]
+        out_ref[at + each : at + GRAM, :] = diagonal if p == 0 else jnp.zeros_like(diagonal)
 
 
 def total_kernel(core_ref, parts_ref, tiles_ref, out_ref):
-    total = jnp.sum(parts_ref[...], axis=0)
-    tiles_ref[...] = jnp.broadcast_to(total[None, BASIS:], tiles_ref.shape)
+    size = BASIS + GRAM
+    pieces = parts_ref.shape[0] // size
+    total = parts_ref[span(0, size), :]
+    for p in range(1, pieces):
+        total = total + parts_ref[span(p, size), :]
+    for p in range(pieces):
+        tiles_ref[span(p, GRAM), :] = total[BASIS:]
     out_ref[...] = jnp.broadcast_to(total[None, :BASIS], out_ref.shape)
+
+
+def unfolded(half_ref):
+    each = GRAM - 1
+    pieces = half_ref.shape[0] // GRAM
+    rows = [half_ref[GRAM * p : GRAM * p + each, :] for p in range(pieces)]
+    step = LANE // each
+    folded, *rest = [jnp.concatenate(rows[step * i : step * (i + 1)], axis=0) for i in range(4)]
+    diagonal = half_ref[each:GRAM, :]
+    row, col = on_diagonal()
+    flipped = folded.T
+    first = jnp.where(row <= col, folded, flipped)
+    second = jnp.where(row == col, diagonal, jnp.where(row > col, folded, flipped))
+    return [first, second, *rest]
 
 
 def inverse_kernel(core_ref, mine_ref, other_ref, inv_ref, work_ref):
     n = inv_ref.shape[0]
     blocks = n // LANE
-    first = core_ref[0] == 0
     work_ref[...] = jnp.zeros_like(work_ref)
+    mine, other = unfolded(mine_ref), unfolded(other_ref)
     for half in range(2):
         for at, place in enumerate(HALVES[half]):
-            if place is not None:
-                mine, other = mine_ref[span(at), :], other_ref[span(at), :]
-                tile = jnp.where(first == (half == 0), mine, other)
-                work_ref[span(place[0]), span(place[1])] = tile
+            tile = jnp.where(core_ref[0] == half, mine[at], other[at])
+            work_ref[span(place[0]), span(place[1])] = tile
     for k in range(blocks):
         done = factor(work_ref[span(k), span(k)])
         row = lax.broadcasted_iota(jnp.int32, done.shape, 0)
@@ -198,6 +231,11 @@
     return lax.all_to_all(pieces, axis, 0, 0, tiled=True)
 
 
+def in_lines(pieces, axis):
+    lines = pieces.reshape(lax.axis_size(axis), 1, -1)
+    return swapped(lines, axis).reshape(pieces.shape)
+
+
 def steps(moves):
     return [(2 * source + c, 2 * target + c) for source, target in moves for c in range(2)]
 
@@ -216,12 +254,15 @@
     mine = mine + lax.ppermute(first, "orb", steps([(0, 7), (3, 2)]))
     other = lax.ppermute(mine, "orb", pairs)
 
-    inner = call(functools.partial(inner_kernel, count=count), [(many, BASIS + GRAM, LANE)], core, mine, other, own)[0]
+    inner = call(
+        functools.partial(inner_kernel, count=count, pieces=many),
+        [(many * (BASIS + GRAM), LANE)], core, mine, other, own,
+    )[0]
     tiles, gram = call(
-        total_kernel, [(many, GRAM, LANE), (many, BASIS, LANE)], core, swapped(inner, "row"),
+        total_kernel, [(many * GRAM, LANE), (many, BASIS, LANE)], core, in_lines(inner, "row"),
         near=(True, False),
     )
-    tiles, gram = lax.optimization_barrier((swapped(tiles, "row").reshape(-1, LANE), gram))
+    tiles, gram = lax.optimization_barrier((in_lines(tiles, "row"), gram))
     gram = swapped(gram, "row")
     others = lax.ppermute(tiles, "orb", pairs)
     inverse = call(

time: 108 us -> 103 us (0.954)
  blocking collectives: 53.7 us -> 50.2 us
  starting transfers between devices: 27.4 us -> 26 us
    all_to_all x2, blocking collectives: 53.7 us -> 50.2 us  [swapped(): return lax.all_to_all(pieces, axis, 0, 0, tiled=True)]
    all_to_all x1, starting transfers between devices: 7.87 us -> 6.42 us  [swapped(): return lax.all_to_all(pieces, axis, 0, 0, tiled=True)]
  transfers between devices with their start and end apart: 7 -> 7, of which waited for: 6 -> 6; matrix products, arithmetic and copies ran while one was open for 0% -> 0% of each run, Pallas kernels for 14% -> 15%
where the time goes in v3:
time: 103 us; the launch traced here: 101 us
  blocking collectives  50.2 us (49%)
  starting transfers between devices  26 us (25%)
  Pallas kernels  17.3 us (17%)
  waiting for transfers between devices  6.32 us (6%)
    all_to_all x2, blocking collectives, swapped(): return lax.all_to_all(pieces, axis, 0, 0, tiled=True)  50.2 us
    pallas_call x5, Pallas kernels, call(): pl.pallas_call(kernel, out_shape=[kind(shape, jnp.float32) for kind, shap...  17.3 us
    ppermute x1, starting transfers between devices, on_device(): lax.ppermute(own, 'orb', steps([(0, 5)]))  7.48 us
    all_to_all x1, starting transfers between devices, swapped(): return lax.all_to_all(pieces, axis, 0, 0, tiled=True)  6.42 us
    ppermute x1, starting transfers between devices, on_device(): others = lax.ppermute(tiles, 'orb', pairs)  4.1 us
    ppermute x1, starting transfers between devices, on_device(): other = lax.ppermute(mine, 'orb', pairs)  4.01 us
  transfers between devices with their start and end apart: 7, of which 6 were waited for; matrix products, arithmetic and copies ran while one was open for 0% of the time, Pallas kernels for 15%

profile of v3, /device:TPU:1, one launch (start us, length us, event | category | flops | bytes accessed | tf_op | source)
XLA Modules:
  0.0 100.9 jit_solution(7514816869947817362)
XLA Ops:
  0.0 7.5 %collective-permute-start.1 = (f32[128,256]{1,0:T(8,128)}, f32[128,256]{1,0:T(8,128)S(1)}, u32[]{:S(2)}, u32[]{:S(2)}) collective-permute-start(f32[128,256]{1,0:T(8,128)} %own_ref.3), channel_id=1, source_target_pairs={{0,10},{1,11},{16,26},{17,27},{32,42},{33,43},{48,58},{49,59},{64,... | collective-permute-start | bytes 393224 | tf_op jit(solution)/shard_map/ppermute | solution.py:251
  7.5 1.3 %collective-permute-start = (f32[128,256]{1,0:T(8,128)}, f32[128,256]{1,0:T(8,128)S(1)}, u32[]{:S(2)}, u32[]{:S(2)}) collective-permute-start(f32[128,256]{1,0:T(8,128)} %own_ref.3), channel_id=1, source_target_pairs={{0,6},{1,7},{16,22},{17,23},{32,38},{33,39},{48,54},{49,55},{64,70... | collective-permute-start | bytes 393224 | tf_op jit(solution)/shard_map/ppermute | solution.py:251
  8.8 1.1 %collective-permute-done.1 = f32[128,256]{1,0:T(8,128)S(1)} collective-permute-done((f32[128,256]{1,0:T(8,128)}, f32[128,256]{1,0:T(8,128)S(1)}, u32[]{:S(2)}, u32[]{:S(2)}) %collective-permute-start.1) | collective-permute-done | bytes 131104 | tf_op jit(solution)/shard_map/ppermute | solution.py:251
  10.0 1.3 %collective-permute-done = f32[128,256]{1,0:T(8,128)S(1)} collective-permute-done((f32[128,256]{1,0:T(8,128)}, f32[128,256]{1,0:T(8,128)S(1)}, u32[]{:S(2)}, u32[]{:S(2)}) %collective-permute-start) | collective-permute-done | bytes 131104 | tf_op jit(solution)/shard_map/ppermute | solution.py:251
  11.3 0.9 add_select_fusion
  12.2 0.0 copy-start
  12.2 1.4 %collective-permute-start.3 = (f32[128,256]{1,0:T(8,128)S(1)}, f32[128,256]{1,0:T(8,128)S(1)}, u32[]{:S(2)}, u32[]{:S(2)}) collective-permute-start(f32[128,256]{1,0:T(8,128)S(1)} %add_select_fusion), channel_id=1, source_target_pairs={{0,14},{1,15},{6,4},{7,5},{16,30},{17,31},{22,20},{23,21},{32,46},... | collective-permute-start | bytes 393224 | tf_op jit(solution)/shard_map/ppermute | solution.py:254
  13.6 1.3 %collective-permute-start.2 = (f32[128,256]{1,0:T(8,128)S(1)}, f32[128,256]{1,0:T(8,128)S(1)}, u32[]{:S(2)}, u32[]{:S(2)}) collective-permute-start(f32[128,256]{1,0:T(8,128)S(1)} %add_select_fusion), channel_id=1, source_target_pairs={{0,2},{1,3},{6,8},{7,9},{10,12},{11,13},{16,18},{17,19},{22,24},{2... | collective-permute-start | bytes 393224 | tf_op jit(solution)/shard_map/ppermute | solution.py:253
  15.0 0.6 collective-permute-done.3
  15.6 1.3 %collective-permute-done.2 = f32[128,256]{1,0:T(8,128)S(1)} collective-permute-done((f32[128,256]{1,0:T(8,128)S(1)}, f32[128,256]{1,0:T(8,128)S(1)}, u32[]{:S(2)}, u32[]{:S(2)}) %collective-permute-start.2) | collective-permute-done | bytes 131104 | tf_op jit(solution)/shard_map/ppermute | solution.py:253
  16.9 4.0 %collective-permute-start.4 = (f32[128,256]{1,0:T(8,128)S(1)}, f32[128,256]{1,0:T(8,128)S(1)}, u32[]{:S(2)}, u32[]{:S(2)}) collective-permute-start(f32[128,256]{1,0:T(8,128)S(1)} %add_add_fusion.mine_ref), channel_id=1, source_target_pairs={{0,1},{1,0},{2,3},{3,2},{4,5},{5,4},{6,7},{7,6},{8,9},{9,8},{10,11... | collective-permute-start | bytes 393224 | tf_op jit(solution)/shard_map/ppermute | solution.py:255
  20.9 1.0 collective-permute-done.4.other_ref
  21.9 0.0 copy-done
  21.9 0.9 shard_map.17
  22.8 31.8 %all_to_all.15 = f32[32,1,6272]{2,1,0:T(1,128)S(1)} all-to-all(f32[32,1,6272]{2,1,0:T(1,128)S(1)} %bitcast.7), channel_id=1, replica_groups=mesh['row'=32,'orb'=16] {'row'}, dimensions={0} | all-to-all | bytes 1605632 | tf_op jit(solution)/shard_map/all_to_all | solution.py:231
  54.7 0.9 shard_map.18
  55.6 18.4 %all_to_all.16 = f32[32,1,2176]{2,1,0:T(1,128)S(1)} all-to-all(f32[32,1,2176]{2,1,0:T(1,128)S(1)} %bitcast.10), channel_id=1, replica_groups=mesh['row'=32,'orb'=16] {'row'}, dimensions={0} | all-to-all | bytes 557056 | tf_op jit(solution)/shard_map/all_to_all | solution.py:231
  74.0 6.4 %all-to-all-start.2 = ((f32[32,32,128]{2,1,0:T(8,128)}), f32[32,32,128]{2,1,0:T(8,128)S(1)}, u32[]{:S(2)}, u32[]{:S(2)}) async-start(f32[32,32,128]{2,1,0:T(8,128)} %get-tuple-element.12), calls=%async_computation.2 | async-start | bytes 1048576 | tf_op jit(solution)/shard_map/all_to_all | solution.py:231
  80.4 4.1 %collective-permute-start.5 = (f32[544,128]{1,0:T(8,128)S(1)}, f32[544,128]{1,0:T(8,128)S(1)}, u32[]{:S(2)}, u32[]{:S(2)}) collective-permute-start(f32[544,128]{1,0:T(8,128)S(1)} %bitcast.8), channel_id=1, source_target_pairs={{0,1},{1,0},{2,3},{3,2},{4,5},{5,4},{6,7},{7,6},{8,9},{9,8},{10,11... | collective-permute-start | bytes 835592 | tf_op jit(solution)/shard_map/ppermute | solution.py:267
  84.5 1.0 collective-permute-done.5.other_ref
  85.5 13.8 %shard_map.19.inv_ref = f32[512,512]{1,0:T(8,128)S(1)} custom-call(s32[1]{0:T(128)} %bitcast.1.core_ref, f32[544,128]{1,0:T(8,128)S(1)} %bitcast.9, f32[544,128]{1,0:T(8,128)S(1)} %collective-permute-done.5.other_ref), custom_call_target="tpu_custom_call" | custom-call | tf_op jit(solution)/shard_map/pallas_call | solution.py:99
  99.4 0.9 shard_map.20.basis_ref
  100.3 0.0 all-to-all-done.2.gram_ref
  100.3 0.7 shard_map.21
  (1 shorter events, 0.0 us)
Async XLA Ops:
  0.0 10.0 %collective-permute-start.1 = (f32[128,256]{1,0:T(8,128)}, f32[128,256]{1,0:T(8,128)S(1)}, u32[]{:S(2)}, u32[]{:S(2)}) collective-permute-start(f32[128,256]{1,0:T(8,128)} %own_ref.3), channel_id=1, source_target_pairs={{0,10},{1,11},{16,26},{17,27},{32,42},{33,43},{48,58},{49,59},{64,... | collective-permute-start | bytes 393224 | tf_op jit(solution)/shard_map/ppermute | solution.py:251
  7.5 3.8 %collective-permute-start = (f32[128,256]{1,0:T(8,128)}, f32[128,256]{1,0:T(8,128)S(1)}, u32[]{:S(2)}, u32[]{:S(2)}) collective-permute-start(f32[128,256]{1,0:T(8,128)} %own_ref.3), channel_id=1, source_target_pairs={{0,6},{1,7},{16,22},{17,23},{32,38},{33,39},{48,54},{49,55},{64,70... | collective-permute-start | bytes 393224 | tf_op jit(solution)/shard_map/ppermute | solution.py:251
  12.2 9.7 %copy-start = (f32[128,256]{1,0:T(8,128)S(1)}, f32[128,256]{1,0:T(8,128)}, u32[]{:S(2)}) copy-start(f32[128,256]{1,0:T(8,128)} %own_ref.3) | copy-start | bytes 393220
  12.2 3.4 %collective-permute-start.3 = (f32[128,256]{1,0:T(8,128)S(1)}, f32[128,256]{1,0:T(8,128)S(1)}, u32[]{:S(2)}, u32[]{:S(2)}) collective-permute-start(f32[128,256]{1,0:T(8,128)S(1)} %add_select_fusion), channel_id=1, source_target_pairs={{0,14},{1,15},{6,4},{7,5},{16,30},{17,31},{22,20},{23,21},{32,46},... | collective-permute-start | bytes 393224 | tf_op jit(solution)/shard_map/ppermute | solution.py:254
  13.6 3.2 %collective-permute-start.2 = (f32[128,256]{1,0:T(8,128)S(1)}, f32[128,256]{1,0:T(8,128)S(1)}, u32[]{:S(2)}, u32[]{:S(2)}) collective-permute-start(f32[128,256]{1,0:T(8,128)S(1)} %add_select_fusion), channel_id=1, source_target_pairs={{0,2},{1,3},{6,8},{7,9},{10,12},{11,13},{16,18},{17,19},{22,24},{2... | collective-permute-start | bytes 393224 | tf_op jit(solution)/shard_map/ppermute | solution.py:253
  16.9 5.0 %collective-permute-start.4 = (f32[128,256]{1,0:T(8,128)S(1)}, f32[128,256]{1,0:T(8,128)S(1)}, u32[]{:S(2)}, u32[]{:S(2)}) collective-permute-start(f32[128,256]{1,0:T(8,128)S(1)} %add_add_fusion.mine_ref), channel_id=1, source_target_pairs={{0,1},{1,0},{2,3},{3,2},{4,5},{5,4},{6,7},{7,6},{8,9},{9,8},{10,11... | collective-permute-start | bytes 393224 | tf_op jit(solution)/shard_map/ppermute | solution.py:255
  74.0 26.3 %all-to-all-start.2 = ((f32[32,32,128]{2,1,0:T(8,128)}), f32[32,32,128]{2,1,0:T(8,128)S(1)}, u32[]{:S(2)}, u32[]{:S(2)}) async-start(f32[32,32,128]{2,1,0:T(8,128)} %get-tuple-element.12), calls=%async_computation.2 | async-start | bytes 1048576 | tf_op jit(solution)/shard_map/all_to_all | solution.py:231
  80.4 5.1 %collective-permute-start.5 = (f32[544,128]{1,0:T(8,128)S(1)}, f32[544,128]{1,0:T(8,128)S(1)}, u32[]{:S(2)}, u32[]{:S(2)}) collective-permute-start(f32[544,128]{1,0:T(8,128)S(1)} %bitcast.8), channel_id=1, source_target_pairs={{0,1},{1,0},{2,3},{3,2},{4,5},{5,4},{6,7},{7,6},{8,9},{9,8},{10,11... | collective-permute-start | bytes 835592 | tf_op jit(solution)/shard_map/ppermute | solution.py:267

commit v4 on v3

--- a/solution.py
+++ b/solution.py
@@ -20,7 +20,14 @@
     )
 
 
-NEAR = 2
+NEAR = 3
+
+
+def inner_sum(left, right):
+    terms = [a * b for a, b in zip(left, right)]
+    while len(terms) > 1:
+        terms = [terms[i] + terms[i + 1] for i in range(0, len(terms), 2)]
+    return terms[0]
 
 
 def factor(block):
@@ -36,11 +43,12 @@
     def pick(vector, i):
         return jnp.take_along_axis(vector, jnp.full(shape, i, jnp.int32), axis=0)
 
+    ahead = None
     for k in range(count):
         base = SUB * k
         inside = (lane >= base) & (lane < base + SUB)
         own = tiles[k]
-        columns = [full(own[:, base + j : base + j + 1]) for j in range(SUB)]
+        columns = ahead or [full(own[:, base + j : base + j + 1]) for j in range(SUB)]
         diag = [[pick(columns[j], i) for j in range(i + 1)] for i in range(SUB)]
         root, low = [], [[None] * SUB for _ in range(SUB)]
         for j in range(SUB):
@@ -67,12 +75,12 @@
         near = range(k + 1, min(k + 1 + NEAR, count))
         far = range(k + 1 + NEAR, count)
         raws = [[full(tiles[t][:, base + j : base + j + 1]) for t in near] for j in range(SUB)]
+        ahead = [full(tiles[t][:, base + SUB + j : base + SUB + j + 1]) for t in near[:1] for j in range(SUB)]
         for i, t in enumerate(near):
             left = solve([raws[j][i] for j in range(SUB)])
-            terms = [left[j] * done[j] for j in range(SUB)]
-            while len(terms) > 1:
-                terms = [terms[m] + terms[m + 1] for m in range(0, len(terms), 2)]
-            tiles[t] = jnp.where(inside, 0.0, tiles[t]) - terms[0]
+            if i == 0:
+                ahead = [c - inner_sum(left, [pick(v, j) for v in left]) for j, c in enumerate(ahead)]
+            tiles[t] = jnp.where(inside, 0.0, tiles[t]) - inner_sum(left, done)
         if far:
             top = row.astype(jnp.bfloat16).astype(jnp.float32)
             mid = (row - top).astype(jnp.bfloat16).astype(jnp.float32)
@@ -178,19 +186,22 @@
             work_ref[span(place[0]), span(place[1])] = tile
     for k in range(blocks):
         done = factor(work_ref[span(k), span(k)])
-        row = lax.broadcasted_iota(jnp.int32, done.shape, 0)
-        col = lax.broadcasted_iota(jnp.int32, done.shape, 1)
+        row, col = on_diagonal()
         done = jnp.where(row >= col, done, 0.0)
-        sides = [slice(0, LANE * k), slice(LANE * (k + 1), n)]
-        for side in sides:
-            if side.start < side.stop:
-                work_ref[span(k), side] = dot(done, work_ref[span(k), side])
+        if k + 1 < blocks:
+            up = dot(done, work_ref[span(k), span(k + 1)])
+            work_ref[span(k + 1), span(k + 1)] = work_ref[span(k + 1), span(k + 1)] - dot(up, up, 0, 0)
+        for j in range(blocks):
+            if j != k:
+                work_ref[span(k), span(j)] = up if j == k + 1 else dot(done, work_ref[span(k), span(j)])
         work_ref[span(k), span(k)] = done
         for i in range(k + 1, blocks):
             up = work_ref[span(k), span(i)]
             work_ref[span(i), span(k)] = jnp.zeros((LANE, LANE), jnp.float32)
-            for side in (slice(LANE * i, n), slice(0, LANE * (k + 1))):
-                work_ref[span(i), side] = work_ref[span(i), side] - dot(up, work_ref[span(k), side], 0, 0)
+            for j in [*range(i, blocks), *range(k + 1)]:
+                if (i, j) != (k + 1, k + 1):
+                    change = dot(up, work_ref[span(k), span(j)], 0, 0)
+                    work_ref[span(i), span(j)] = work_ref[span(i), span(j)] - change
     for i in range(blocks):
         split = LANE * (i + 1)
         inv_ref[span(i), :split] = work_ref[span(i), :split]

time: 103 us -> 101 us (0.981)
  Pallas kernels: 17.3 us -> 15.7 us
    pallas_call x5, Pallas kernels: 17.3 us -> 15.7 us  [call(): pl.pallas_call(kernel, out_shape=[kind(shape, jnp.float32) for kind, shap...]
  transfers between devices with their start and end apart: 7 -> 7, of which waited for: 6 -> 6; matrix products, arithmetic and copies ran while one was open for 0% -> 0% of each run, Pallas kernels for 15% -> 13%
where the time goes in v4:
time: 101 us; the launch traced here: 99.4 us
  blocking collectives  50.2 us (50%)
  starting transfers between devices  26 us (26%)
  Pallas kernels  15.7 us (16%)
  waiting for transfers between devices  6.32 us (6%)
    all_to_all x2, blocking collectives, swapped(): return lax.all_to_all(pieces, axis, 0, 0, tiled=True)  50.2 us
    pallas_call x5, Pallas kernels, call(): pl.pallas_call(kernel, out_shape=[kind(shape, jnp.float32) for kind, shap...  15.7 us
    ppermute x1, starting transfers between devices, on_device(): lax.ppermute(own, 'orb', steps([(0, 5)]))  7.48 us
    all_to_all x1, starting transfers between devices, swapped(): return lax.all_to_all(pieces, axis, 0, 0, tiled=True)  6.42 us
    ppermute x1, starting transfers between devices, on_device(): others = lax.ppermute(tiles, 'orb', pairs)  4.1 us
    ppermute x1, starting transfers between devices, on_device(): other = lax.ppermute(mine, 'orb', pairs)  4.01 us
  transfers between devices with their start and end apart: 7, of which 6 were waited for; matrix products, arithmetic and copies ran while one was open for 0% of the time, Pallas kernels for 13%

profile of v4, /device:TPU:1, one launch (start us, length us, event | category | flops | bytes accessed | tf_op | source)
XLA Modules:
  0.0 99.4 jit_solution(6545389646123488431)
XLA Ops:
  0.0 7.5 %collective-permute-start.1 = (f32[128,256]{1,0:T(8,128)}, f32[128,256]{1,0:T(8,128)S(1)}, u32[]{:S(2)}, u32[]{:S(2)}) collective-permute-start(f32[128,256]{1,0:T(8,128)} %own_ref.3), channel_id=1, source_target_pairs={{0,10},{1,11},{16,26},{17,27},{32,42},{33,43},{48,58},{49,59},{64,... | collective-permute-start | bytes 393224 | tf_op jit(solution)/shard_map/ppermute | solution.py:262
  7.5 1.3 %collective-permute-start = (f32[128,256]{1,0:T(8,128)}, f32[128,256]{1,0:T(8,128)S(1)}, u32[]{:S(2)}, u32[]{:S(2)}) collective-permute-start(f32[128,256]{1,0:T(8,128)} %own_ref.3), channel_id=1, source_target_pairs={{0,6},{1,7},{16,22},{17,23},{32,38},{33,39},{48,54},{49,55},{64,70... | collective-permute-start | bytes 393224 | tf_op jit(solution)/shard_map/ppermute | solution.py:262
  8.8 1.1 %collective-permute-done.1 = f32[128,256]{1,0:T(8,128)S(1)} collective-permute-done((f32[128,256]{1,0:T(8,128)}, f32[128,256]{1,0:T(8,128)S(1)}, u32[]{:S(2)}, u32[]{:S(2)}) %collective-permute-start.1) | collective-permute-done | bytes 131104 | tf_op jit(solution)/shard_map/ppermute | solution.py:262
  10.0 1.3 %collective-permute-done = f32[128,256]{1,0:T(8,128)S(1)} collective-permute-done((f32[128,256]{1,0:T(8,128)}, f32[128,256]{1,0:T(8,128)S(1)}, u32[]{:S(2)}, u32[]{:S(2)}) %collective-permute-start) | collective-permute-done | bytes 131104 | tf_op jit(solution)/shard_map/ppermute | solution.py:262
  11.3 0.9 add_select_fusion
  12.2 0.0 copy-start
  12.2 1.4 %collective-permute-start.3 = (f32[128,256]{1,0:T(8,128)S(1)}, f32[128,256]{1,0:T(8,128)S(1)}, u32[]{:S(2)}, u32[]{:S(2)}) collective-permute-start(f32[128,256]{1,0:T(8,128)S(1)} %add_select_fusion), channel_id=1, source_target_pairs={{0,14},{1,15},{6,4},{7,5},{16,30},{17,31},{22,20},{23,21},{32,46},... | collective-permute-start | bytes 393224 | tf_op jit(solution)/shard_map/ppermute | solution.py:265
  13.6 1.3 %collective-permute-start.2 = (f32[128,256]{1,0:T(8,128)S(1)}, f32[128,256]{1,0:T(8,128)S(1)}, u32[]{:S(2)}, u32[]{:S(2)}) collective-permute-start(f32[128,256]{1,0:T(8,128)S(1)} %add_select_fusion), channel_id=1, source_target_pairs={{0,2},{1,3},{6,8},{7,9},{10,12},{11,13},{16,18},{17,19},{22,24},{2... | collective-permute-start | bytes 393224 | tf_op jit(solution)/shard_map/ppermute | solution.py:264
  15.0 0.6 collective-permute-done.3
  15.6 1.3 %collective-permute-done.2 = f32[128,256]{1,0:T(8,128)S(1)} collective-permute-done((f32[128,256]{1,0:T(8,128)S(1)}, f32[128,256]{1,0:T(8,128)S(1)}, u32[]{:S(2)}, u32[]{:S(2)}) %collective-permute-start.2) | collective-permute-done | bytes 131104 | tf_op jit(solution)/shard_map/ppermute | solution.py:264
  16.9 4.0 %collective-permute-start.4 = (f32[128,256]{1,0:T(8,128)S(1)}, f32[128,256]{1,0:T(8,128)S(1)}, u32[]{:S(2)}, u32[]{:S(2)}) collective-permute-start(f32[128,256]{1,0:T(8,128)S(1)} %add_add_fusion.mine_ref), channel_id=1, source_target_pairs={{0,1},{1,0},{2,3},{3,2},{4,5},{5,4},{6,7},{7,6},{8,9},{9,8},{10,11... | collective-permute-start | bytes 393224 | tf_op jit(solution)/shard_map/ppermute | solution.py:266
  20.9 1.0 collective-permute-done.4.other_ref
  21.9 0.0 copy-done
  21.9 0.9 shard_map.17
  22.8 31.8 %all_to_all.15 = f32[32,1,6272]{2,1,0:T(1,128)S(1)} all-to-all(f32[32,1,6272]{2,1,0:T(1,128)S(1)} %bitcast.7), channel_id=1, replica_groups=mesh['row'=32,'orb'=16] {'row'}, dimensions={0} | all-to-all | bytes 1605632 | tf_op jit(solution)/shard_map/all_to_all | solution.py:242
  54.7 0.9 shard_map.18
  55.6 18.4 %all_to_all.16 = f32[32,1,2176]{2,1,0:T(1,128)S(1)} all-to-all(f32[32,1,2176]{2,1,0:T(1,128)S(1)} %bitcast.10), channel_id=1, replica_groups=mesh['row'=32,'orb'=16] {'row'}, dimensions={0} | all-to-all | bytes 557056 | tf_op jit(solution)/shard_map/all_to_all | solution.py:242
  74.0 6.4 %all-to-all-start.2 = ((f32[32,32,128]{2,1,0:T(8,128)}), f32[32,32,128]{2,1,0:T(8,128)S(1)}, u32[]{:S(2)}, u32[]{:S(2)}) async-start(f32[32,32,128]{2,1,0:T(8,128)} %get-tuple-element.12), calls=%async_computation.2 | async-start | bytes 1048576 | tf_op jit(solution)/shard_map/all_to_all | solution.py:242
  80.4 4.1 %collective-permute-start.5 = (f32[544,128]{1,0:T(8,128)S(1)}, f32[544,128]{1,0:T(8,128)S(1)}, u32[]{:S(2)}, u32[]{:S(2)}) collective-permute-start(f32[544,128]{1,0:T(8,128)S(1)} %bitcast.8), channel_id=1, source_target_pairs={{0,1},{1,0},{2,3},{3,2},{4,5},{5,4},{6,7},{7,6},{8,9},{9,8},{10,11... | collective-permute-start | bytes 835592 | tf_op jit(solution)/shard_map/ppermute | solution.py:278
  84.5 1.0 collective-permute-done.5.other_ref
  85.5 12.3 %shard_map.19.inv_ref = f32[512,512]{1,0:T(8,128)S(1)} custom-call(s32[1]{0:T(128)} %bitcast.1.core_ref, f32[544,128]{1,0:T(8,128)S(1)} %bitcast.9, f32[544,128]{1,0:T(8,128)S(1)} %collective-permute-done.5.other_ref), custom_call_target="tpu_custom_call" | custom-call | tf_op jit(solution)/shard_map/pallas_call | solution.py:107
  97.8 0.9 shard_map.20.basis_ref
  98.7 0.0 all-to-all-done.2.gram_ref
  98.7 0.7 shard_map.21
  (1 shorter events, 0.0 us)
Async XLA Ops:
  0.0 10.0 %collective-permute-start.1 = (f32[128,256]{1,0:T(8,128)}, f32[128,256]{1,0:T(8,128)S(1)}, u32[]{:S(2)}, u32[]{:S(2)}) collective-permute-start(f32[128,256]{1,0:T(8,128)} %own_ref.3), channel_id=1, source_target_pairs={{0,10},{1,11},{16,26},{17,27},{32,42},{33,43},{48,58},{49,59},{64,... | collective-permute-start | bytes 393224 | tf_op jit(solution)/shard_map/ppermute | solution.py:262
  7.5 3.8 %collective-permute-start = (f32[128,256]{1,0:T(8,128)}, f32[128,256]{1,0:T(8,128)S(1)}, u32[]{:S(2)}, u32[]{:S(2)}) collective-permute-start(f32[128,256]{1,0:T(8,128)} %own_ref.3), channel_id=1, source_target_pairs={{0,6},{1,7},{16,22},{17,23},{32,38},{33,39},{48,54},{49,55},{64,70... | collective-permute-start | bytes 393224 | tf_op jit(solution)/shard_map/ppermute | solution.py:262
  12.2 9.7 %copy-start = (f32[128,256]{1,0:T(8,128)S(1)}, f32[128,256]{1,0:T(8,128)}, u32[]{:S(2)}) copy-start(f32[128,256]{1,0:T(8,128)} %own_ref.3) | copy-start | bytes 393220
  12.2 3.4 %collective-permute-start.3 = (f32[128,256]{1,0:T(8,128)S(1)}, f32[128,256]{1,0:T(8,128)S(1)}, u32[]{:S(2)}, u32[]{:S(2)}) collective-permute-start(f32[128,256]{1,0:T(8,128)S(1)} %add_select_fusion), channel_id=1, source_target_pairs={{0,14},{1,15},{6,4},{7,5},{16,30},{17,31},{22,20},{23,21},{32,46},... | collective-permute-start | bytes 393224 | tf_op jit(solution)/shard_map/ppermute | solution.py:265
  13.6 3.2 %collective-permute-start.2 = (f32[128,256]{1,0:T(8,128)S(1)}, f32[128,256]{1,0:T(8,128)S(1)}, u32[]{:S(2)}, u32[]{:S(2)}) collective-permute-start(f32[128,256]{1,0:T(8,128)S(1)} %add_select_fusion), channel_id=1, source_target_pairs={{0,2},{1,3},{6,8},{7,9},{10,12},{11,13},{16,18},{17,19},{22,24},{2... | collective-permute-start | bytes 393224 | tf_op jit(solution)/shard_map/ppermute | solution.py:264
  16.9 5.0 %collective-permute-start.4 = (f32[128,256]{1,0:T(8,128)S(1)}, f32[128,256]{1,0:T(8,128)S(1)}, u32[]{:S(2)}, u32[]{:S(2)}) collective-permute-start(f32[128,256]{1,0:T(8,128)S(1)} %add_add_fusion.mine_ref), channel_id=1, source_target_pairs={{0,1},{1,0},{2,3},{3,2},{4,5},{5,4},{6,7},{7,6},{8,9},{9,8},{10,11... | collective-permute-start | bytes 393224 | tf_op jit(solution)/shard_map/ppermute | solution.py:266
  74.0 24.7 %all-to-all-start.2 = ((f32[32,32,128]{2,1,0:T(8,128)}), f32[32,32,128]{2,1,0:T(8,128)S(1)}, u32[]{:S(2)}, u32[]{:S(2)}) async-start(f32[32,32,128]{2,1,0:T(8,128)} %get-tuple-element.12), calls=%async_computation.2 | async-start | bytes 1048576 | tf_op jit(solution)/shard_map/all_to_all | solution.py:242
  80.4 5.1 %collective-permute-start.5 = (f32[544,128]{1,0:T(8,128)S(1)}, f32[544,128]{1,0:T(8,128)S(1)}, u32[]{:S(2)}, u32[]{:S(2)}) collective-permute-start(f32[544,128]{1,0:T(8,128)S(1)} %bitcast.8), channel_id=1, source_target_pairs={{0,1},{1,0},{2,3},{3,2},{4,5},{5,4},{6,7},{7,6},{8,9},{9,8},{10,11... | collective-permute-start | bytes 835592 | tf_op jit(solution)/shard_map/ppermute | solution.py:278

commit v5 on v4

--- a/solution.py
+++ b/solution.py
@@ -175,14 +175,17 @@
     return [first, second, *rest]
 
 
-def inverse_kernel(core_ref, mine_ref, other_ref, inv_ref, work_ref):
-    n = inv_ref.shape[0]
+def basis_kernel(index_ref, near_ref, far_ref, mine_ref, other_ref, basis_ref, work_ref, raw_ref, q_ref):
+    n, width = work_ref.shape[0], near_ref.shape[1]
     blocks = n // LANE
+    core = index_ref[0] % 2
+    raw_ref[:, :width], raw_ref[:, width:] = raw_blocks(core, near_ref, far_ref)
+    basis_ref[...] = jnp.zeros_like(basis_ref)
     work_ref[...] = jnp.zeros_like(work_ref)
     mine, other = unfolded(mine_ref), unfolded(other_ref)
     for half in range(2):
         for at, place in enumerate(HALVES[half]):
-            tile = jnp.where(core_ref[0] == half, mine[at], other[at])
+            tile = jnp.where(core == half, mine[at], other[at])
             work_ref[span(place[0]), span(place[1])] = tile
     for k in range(blocks):
         done = factor(work_ref[span(k), span(k)])
@@ -202,25 +205,14 @@
                 if (i, j) != (k + 1, k + 1):
                     change = dot(up, work_ref[span(k), span(j)], 0, 0)
                     work_ref[span(i), span(j)] = work_ref[span(i), span(j)] - change
-    for i in range(blocks):
-        split = LANE * (i + 1)
-        inv_ref[span(i), :split] = work_ref[span(i), :split]
-        if split < n:
-            inv_ref[span(i), split:] = jnp.zeros((LANE, n - split), jnp.float32)
-
-
-def basis_kernel(index_ref, mine_ref, other_ref, inv_ref, basis_ref):
-    zero, one = raw_blocks(index_ref[0] % 2, mine_ref, other_ref)
-    width = zero.shape[1]
-    top = dot(zero, inv_ref[:width, :width], 1, 1)
-    low = dot(zero, inv_ref[width:, :width], 1, 1) + dot(one, inv_ref[width:, width:], 1, 1)
-    basis_ref[:, :width] = jnp.where(index_ref[0] == 1, low, top)
-    basis_ref[:, width:] = low
-
-    @pl.when(index_ref[0] > 1)
+        known = slice(0, LANE * (k + 1))
+        part = dot(raw_ref[:, known], work_ref[span(k), known], 1, 1)
+        q_ref[:, span(k)] = part
+        basis_ref[:, known] = basis_ref[:, known] + dot(part, work_ref[span(k), known])
+
+    @pl.when(index_ref[0] < 2)
     def _():
-        basis_ref[:, :width] = dot(top, inv_ref[:width, :width]) + dot(low, inv_ref[width:, :width])
-        basis_ref[:, width:] = dot(low, inv_ref[width:, width:])
+        basis_ref[:, :width] = jnp.where(core == 0, q_ref[:, :width], q_ref[:, width:])
 
 
 def finish_kernel(index_ref, basis_ref, gram_ref, own_ref, out_ref):
@@ -259,10 +251,9 @@
     core, chip = index % 2, index // 2
     pairs = [(i, i ^ 1) for i in range(groups)]
 
-    first = lax.ppermute(own, "orb", steps([(0, 3)])) + lax.ppermute(own, "orb", steps([(0, 5)]))
-    first = jnp.where(chip == 0, own, first)
-    mine = first + lax.ppermute(first, "orb", steps([(0, 1), (3, 4), (5, 6)]))
-    mine = mine + lax.ppermute(first, "orb", steps([(0, 7), (3, 2)]))
+    given = [lax.ppermute(own, "orb", steps([(0, target)])) for target in (5, 3, 7, 1)]
+    first = jnp.where(chip == 0, own, (given[0] + given[1]) + (given[2] + given[3]))
+    mine = first + lax.ppermute(first, "orb", steps([(1, 2), (3, 4), (5, 6)]))
     other = lax.ppermute(mine, "orb", pairs)
 
     inner = call(
@@ -276,11 +267,10 @@
     tiles, gram = lax.optimization_barrier((in_lines(tiles, "row"), gram))
     gram = swapped(gram, "row")
     others = lax.ppermute(tiles, "orb", pairs)
-    inverse = call(
-        inverse_kernel, [(2 * width, 2 * width)], core, tiles, others,
-        scratch=[(2 * width, 2 * width)],
+    basis = call(
+        basis_kernel, [(rows, 2 * width)], index, mine, other, tiles, others,
+        scratch=[(2 * width, 2 * width)] + [(rows, 2 * width)] * 2,
     )[0]
-    basis = call(basis_kernel, [(rows, 2 * width)], index, mine, other, inverse)[0]
     return call(finish_kernel, [own.shape], index, basis, gram, own, near=(False,))[0]
 
 

time: 101 us -> 102 us (level)
  the two profiles are of different devices: /device:TPU:1 before, /device:TPU:51 now
where the time goes in v5:
time: 102 us; the launch traced here: 101 us
  blocking collectives  49.6 us (49%)
  starting transfers between devices  19.9 us (20%)
  Pallas kernels  17.6 us (17%)
  waiting for transfers between devices  14.1 us (14%)
    all_to_all x2, blocking collectives, swapped(): return lax.all_to_all(pieces, axis, 0, 0, tiled=True)  49.6 us
    pallas_call x4, Pallas kernels, call(): pl.pallas_call(kernel, out_shape=[kind(shape, jnp.float32) for kind, shap...  17.6 us
    ppermute x1, waiting for transfers between devices, on_device(): mine = first + lax.ppermute(first, 'orb', steps([(1, 2), (3, 4), (5, 6)]))  12.2 us
    all_to_all x1, starting transfers between devices, swapped(): return lax.all_to_all(pieces, axis, 0, 0, tiled=True)  7.12 us
    ppermute x1, starting transfers between devices, on_device(): others = lax.ppermute(tiles, 'orb', pairs)  4.38 us
    ppermute x1, starting transfers between devices, on_device(): other = lax.ppermute(mine, 'orb', pairs)  4.31 us
    ppermute x4, starting transfers between devices, on_device(): lax.ppermute(own, 'orb', steps([(0, target)]))  2.66 us
  transfers between devices with their start and end apart: 8, of which 3 were waited for; matrix products, arithmetic and copies ran while one was open for 0% of the time, Pallas kernels for 14%

profile of v5, /device:TPU:51, one launch (start us, length us, event | category | flops | bytes accessed | tf_op | source)
XLA Modules:
  0.0 101.4 jit_solution(3494411519986742361)
XLA Ops:
  0.0 0.7 collective-permute-start.3
  0.7 0.7 collective-permute-start.2
  1.3 0.7 collective-permute-start.1
  2.0 0.7 collective-permute-start
  2.7 0.0 collective-permute-done.3
  2.7 0.0 collective-permute-done.2
  2.7 0.0 collective-permute-done.1
  2.7 0.0 collective-permute-done
  2.8 0.1 add_select_fusion
  2.8 0.0 copy-start
  2.8 1.4 %collective-permute-start.4 = (f32[128,256]{1,0:T(8,128)S(1)}, f32[128,256]{1,0:T(8,128)S(1)}, u32[]{:S(2)}, u32[]{:S(2)}) collective-permute-start(f32[128,256]{1,0:T(8,128)S(1)} %add_select_fusion), channel_id=1, source_target_pairs={{2,4},{3,5},{6,8},{7,9},{10,12},{11,13},{18,20},{19,21},{22,24},{2... | collective-permute-start | bytes 393224 | tf_op jit(solution)/shard_map/ppermute | solution.py:256
  4.3 12.2 %collective-permute-done.4 = f32[128,256]{1,0:T(8,128)S(1)} collective-permute-done((f32[128,256]{1,0:T(8,128)S(1)}, f32[128,256]{1,0:T(8,128)S(1)}, u32[]{:S(2)}, u32[]{:S(2)}) %collective-permute-start.4) | collective-permute-done | bytes 131104 | tf_op jit(solution)/shard_map/ppermute | solution.py:256
  16.4 4.3 %collective-permute-start.5 = (f32[128,256]{1,0:T(8,128)S(1)}, f32[128,256]{1,0:T(8,128)S(1)}, u32[]{:S(2)}, u32[]{:S(2)}) collective-permute-start(f32[128,256]{1,0:T(8,128)S(1)} %add.20.mine_ref.near_ref), channel_id=1, source_target_pairs={{0,1},{1,0},{2,3},{3,2},{4,5},{5,4},{6,7},{7,6},{8,9},{9,8},{10,11... | collective-permute-start | bytes 393224 | tf_op jit(solution)/shard_map/ppermute | solution.py:257
  20.8 1.0 collective-permute-done.5.other_ref.far_ref
  21.7 0.0 copy-done
  21.7 0.9 shard_map.17
  22.7 31.6 %all_to_all.15 = f32[32,1,6272]{2,1,0:T(1,128)S(1)} all-to-all(f32[32,1,6272]{2,1,0:T(1,128)S(1)} %bitcast.7), channel_id=1, replica_groups=mesh['row'=32,'orb'=16] {'row'}, dimensions={0} | all-to-all | bytes 1605632 | tf_op jit(solution)/shard_map/all_to_all | solution.py:234
  54.3 0.9 shard_map.18
  55.1 18.0 %all_to_all.16 = f32[32,1,2176]{2,1,0:T(1,128)S(1)} all-to-all(f32[32,1,2176]{2,1,0:T(1,128)S(1)} %bitcast.10), channel_id=1, replica_groups=mesh['row'=32,'orb'=16] {'row'}, dimensions={0} | all-to-all | bytes 557056 | tf_op jit(solution)/shard_map/all_to_all | solution.py:234
  73.1 7.1 %all-to-all-start.2 = ((f32[32,32,128]{2,1,0:T(8,128)}), f32[32,32,128]{2,1,0:T(8,128)S(1)}, u32[]{:S(2)}, u32[]{:S(2)}) async-start(f32[32,32,128]{2,1,0:T(8,128)} %get-tuple-element.12), calls=%async_computation.2 | async-start | bytes 1048576 | tf_op jit(solution)/shard_map/all_to_all | solution.py:234
  80.3 4.4 %collective-permute-start.6 = (f32[544,128]{1,0:T(8,128)S(1)}, f32[544,128]{1,0:T(8,128)S(1)}, u32[]{:S(2)}, u32[]{:S(2)}) collective-permute-start(f32[544,128]{1,0:T(8,128)S(1)} %bitcast.8), channel_id=1, source_target_pairs={{0,1},{1,0},{2,3},{3,2},{4,5},{5,4},{6,7},{7,6},{8,9},{9,8},{10,11... | collective-permute-start | bytes 835592 | tf_op jit(solution)/shard_map/ppermute | solution.py:269
  84.6 1.0 collective-permute-done.6.other_ref
  85.6 14.5 %shard_map.19.basis_ref = f32[128,512]{1,0:T(8,128)S(1)} custom-call(s32[1]{0:T(128)} %bitcast.index_ref, f32[128,256]{1,0:T(8,128)S(1)} %add.20.mine_ref.near_ref, f32[128,256]{1,0:T(8,128)S(1)} %collective-permute-done.5.other_ref.far_ref, f32[544,128]{1,0:T(8,128)S(1)} %bitcast.9, f32[544,128]{1,0:T(8,128)S(1)} %collective-permute-done.6.other_ref), custom_call_target="tpu_custom_call" | custom-call | tf_op jit(solution)/shard_map/pallas_call | solution.py:107
  100.1 0.0 all-to-all-done.2.gram_ref
  100.1 1.3 %shard_map.20 = f32[128,256]{1,0:T(8,128)} custom-call(s32[1]{0:T(128)} %bitcast.index_ref, f32[128,512]{1,0:T(8,128)S(1)} %shard_map.19.basis_ref, f32[32,32,128]{2,1,0:T(8,128)S(1)} %all-to-all-done.2.gram_ref, f32[128,256]{1,0:T(8,128)S(1)} %copy-done), custom_call_target="tpu_custom_call" | custom-call | tf_op jit(solution)/shard_map/pallas_call | solution.py:107
  (1 shorter events, 0.0 us)
Async XLA Ops:
  0.0 2.7 %collective-permute-start.3 = (f32[128,256]{1,0:T(8,128)}, f32[128,256]{1,0:T(8,128)S(1)}, u32[]{:S(2)}, u32[]{:S(2)}) collective-permute-start(f32[128,256]{1,0:T(8,128)} %own_ref.3), channel_id=1, source_target_pairs={{0,2},{1,3},{16,18},{17,19},{32,34},{33,35},{48,50},{49,51},{64,66... | collective-permute-start | bytes 393224 | tf_op jit(solution)/shard_map/ppermute | solution.py:254
  0.7 2.1 %collective-permute-start.2 = (f32[128,256]{1,0:T(8,128)}, f32[128,256]{1,0:T(8,128)S(1)}, u32[]{:S(2)}, u32[]{:S(2)}) collective-permute-start(f32[128,256]{1,0:T(8,128)} %own_ref.3), channel_id=1, source_target_pairs={{0,14},{1,15},{16,30},{17,31},{32,46},{33,47},{48,62},{49,63},{64,... | collective-permute-start | bytes 393224 | tf_op jit(solution)/shard_map/ppermute | solution.py:254
  1.3 1.4 %collective-permute-start.1 = (f32[128,256]{1,0:T(8,128)}, f32[128,256]{1,0:T(8,128)S(1)}, u32[]{:S(2)}, u32[]{:S(2)}) collective-permute-start(f32[128,256]{1,0:T(8,128)} %own_ref.3), channel_id=1, source_target_pairs={{0,6},{1,7},{16,22},{17,23},{32,38},{33,39},{48,54},{49,55},{64,70... | collective-permute-start | bytes 393224 | tf_op jit(solution)/shard_map/ppermute | solution.py:254
  2.0 0.7 collective-permute-start
  2.8 18.9 %copy-start = (f32[128,256]{1,0:T(8,128)S(1)}, f32[128,256]{1,0:T(8,128)}, u32[]{:S(2)}) copy-start(f32[128,256]{1,0:T(8,128)} %own_ref.3) | copy-start | bytes 393220
  2.8 13.6 %collective-permute-start.4 = (f32[128,256]{1,0:T(8,128)S(1)}, f32[128,256]{1,0:T(8,128)S(1)}, u32[]{:S(2)}, u32[]{:S(2)}) collective-permute-start(f32[128,256]{1,0:T(8,128)S(1)} %add_select_fusion), channel_id=1, source_target_pairs={{2,4},{3,5},{6,8},{7,9},{10,12},{11,13},{18,20},{19,21},{22,24},{2... | collective-permute-start | bytes 393224 | tf_op jit(solution)/shard_map/ppermute | solution.py:256
  16.4 5.3 %collective-permute-start.5 = (f32[128,256]{1,0:T(8,128)S(1)}, f32[128,256]{1,0:T(8,128)S(1)}, u32[]{:S(2)}, u32[]{:S(2)}) collective-permute-start(f32[128,256]{1,0:T(8,128)S(1)} %add.20.mine_ref.near_ref), channel_id=1, source_target_pairs={{0,1},{1,0},{2,3},{3,2},{4,5},{5,4},{6,7},{7,6},{8,9},{9,8},{10,11... | collective-permute-start | bytes 393224 | tf_op jit(solution)/shard_map/ppermute | solution.py:257
  73.1 27.0 %all-to-all-start.2 = ((f32[32,32,128]{2,1,0:T(8,128)}), f32[32,32,128]{2,1,0:T(8,128)S(1)}, u32[]{:S(2)}, u32[]{:S(2)}) async-start(f32[32,32,128]{2,1,0:T(8,128)} %get-tuple-element.12), calls=%async_computation.2 | async-start | bytes 1048576 | tf_op jit(solution)/shard_map/all_to_all | solution.py:234
  80.3 5.4 %collective-permute-start.6 = (f32[544,128]{1,0:T(8,128)S(1)}, f32[544,128]{1,0:T(8,128)S(1)}, u32[]{:S(2)}, u32[]{:S(2)}) collective-permute-start(f32[544,128]{1,0:T(8,128)S(1)} %bitcast.8), channel_id=1, source_target_pairs={{0,1},{1,0},{2,3},{3,2},{4,5},{5,4},{6,7},{7,6},{8,9},{9,8},{10,11... | collective-permute-start | bytes 835592 | tf_op jit(solution)/shard_map/ppermute | solution.py:269

commit v6 on v4

--- a/solution.py
+++ b/solution.py
@@ -259,10 +259,9 @@
     core, chip = index % 2, index // 2
     pairs = [(i, i ^ 1) for i in range(groups)]
 
-    first = lax.ppermute(own, "orb", steps([(0, 3)])) + lax.ppermute(own, "orb", steps([(0, 5)]))
-    first = jnp.where(chip == 0, own, first)
-    mine = first + lax.ppermute(first, "orb", steps([(0, 1), (3, 4), (5, 6)]))
-    mine = mine + lax.ppermute(first, "orb", steps([(0, 7), (3, 2)]))
+    given = [lax.ppermute(own, "orb", steps([(0, target)])) for target in (5, 7, 3, 1)]
+    first = jnp.where(chip == 0, own, (given[0] + given[1]) + (given[2] + given[3]))
+    mine = first + lax.ppermute(first, "orb", steps([(1, 2), (3, 4), (7, 6)]))
     other = lax.ppermute(mine, "orb", pairs)
 
     inner = call(

time: 101 us -> 99.8 us (0.988)
  the two profiles are of different devices: /device:TPU:1 before, /device:TPU:51 now
where the time goes in v6:
time: 99.8 us; the launch traced here: 99.4 us
  blocking collectives  49.6 us (50%)
  starting transfers between devices  20.1 us (20%)
  Pallas kernels  16.8 us (17%)
  waiting for transfers between devices  12.7 us (13%)
    all_to_all x2, blocking collectives, swapped(): return lax.all_to_all(pieces, axis, 0, 0, tiled=True)  49.6 us
    pallas_call x5, Pallas kernels, call(): pl.pallas_call(kernel, out_shape=[kind(shape, jnp.float32) for kind, shap...  16.8 us
    ppermute x1, waiting for transfers between devices, on_device(): mine = first + lax.ppermute(first, 'orb', steps([(1, 2), (3, 4), (7, 6)]))  10.7 us
    all_to_all x1, starting transfers between devices, swapped(): return lax.all_to_all(pieces, axis, 0, 0, tiled=True)  7.12 us
    ppermute x1, starting transfers between devices, on_device(): other = lax.ppermute(mine, 'orb', pairs)  4.5 us
    ppermute x1, starting transfers between devices, on_device(): others = lax.ppermute(tiles, 'orb', pairs)  4.38 us
    ppermute x4, starting transfers between devices, on_device(): lax.ppermute(own, 'orb', steps([(0, target)]))  2.66 us
  transfers between devices with their start and end apart: 8, of which 3 were waited for; matrix products, arithmetic and copies ran while one was open for 0% of the time, Pallas kernels for 14%

profile of v6, /device:TPU:51, one launch (start us, length us, event | category | flops | bytes accessed | tf_op | source)
XLA Modules:
  0.0 99.4 jit_solution(1016794749648622172)
XLA Ops:
  0.0 0.7 collective-permute-start.3
  0.7 0.7 collective-permute-start.2
  1.3 0.7 collective-permute-start.1
  2.0 0.7 collective-permute-start
  2.7 0.0 collective-permute-done.3
  2.7 0.0 collective-permute-done.2
  2.7 0.0 collective-permute-done.1
  2.7 0.0 collective-permute-done
  2.8 0.1 add_select_fusion
  2.8 0.0 copy-start
  2.8 1.4 %collective-permute-start.4 = (f32[128,256]{1,0:T(8,128)S(1)}, f32[128,256]{1,0:T(8,128)S(1)}, u32[]{:S(2)}, u32[]{:S(2)}) collective-permute-start(f32[128,256]{1,0:T(8,128)S(1)} %add_select_fusion), channel_id=1, source_target_pairs={{2,4},{3,5},{6,8},{7,9},{14,12},{15,13},{18,20},{19,21},{22,24},{2... | collective-permute-start | bytes 393224 | tf_op jit(solution)/shard_map/ppermute | solution.py:264
  4.3 10.7 %collective-permute-done.4 = f32[128,256]{1,0:T(8,128)S(1)} collective-permute-done((f32[128,256]{1,0:T(8,128)S(1)}, f32[128,256]{1,0:T(8,128)S(1)}, u32[]{:S(2)}, u32[]{:S(2)}) %collective-permute-start.4) | collective-permute-done | bytes 131104 | tf_op jit(solution)/shard_map/ppermute | solution.py:264
  15.0 4.5 %collective-permute-start.5 = (f32[128,256]{1,0:T(8,128)S(1)}, f32[128,256]{1,0:T(8,128)S(1)}, u32[]{:S(2)}, u32[]{:S(2)}) collective-permute-start(f32[128,256]{1,0:T(8,128)S(1)} %add.20.mine_ref), channel_id=1, source_target_pairs={{0,1},{1,0},{2,3},{3,2},{4,5},{5,4},{6,7},{7,6},{8,9},{9,8},{10,11... | collective-permute-start | bytes 393224 | tf_op jit(solution)/shard_map/ppermute | solution.py:265
  19.5 1.0 collective-permute-done.5.other_ref
  20.5 0.0 copy-done
  20.5 1.0 shard_map.17
  21.4 31.6 %all_to_all.15 = f32[32,1,6272]{2,1,0:T(1,128)S(1)} all-to-all(f32[32,1,6272]{2,1,0:T(1,128)S(1)} %bitcast.7), channel_id=1, replica_groups=mesh['row'=32,'orb'=16] {'row'}, dimensions={0} | all-to-all | bytes 1605632 | tf_op jit(solution)/shard_map/all_to_all | solution.py:242
  53.0 0.9 shard_map.18
  53.9 18.0 %all_to_all.16 = f32[32,1,2176]{2,1,0:T(1,128)S(1)} all-to-all(f32[32,1,2176]{2,1,0:T(1,128)S(1)} %bitcast.10), channel_id=1, replica_groups=mesh['row'=32,'orb'=16] {'row'}, dimensions={0} | all-to-all | bytes 557056 | tf_op jit(solution)/shard_map/all_to_all | solution.py:242
  71.9 7.1 %all-to-all-start.2 = ((f32[32,32,128]{2,1,0:T(8,128)}), f32[32,32,128]{2,1,0:T(8,128)S(1)}, u32[]{:S(2)}, u32[]{:S(2)}) async-start(f32[32,32,128]{2,1,0:T(8,128)} %get-tuple-element.12), calls=%async_computation.2 | async-start | bytes 1048576 | tf_op jit(solution)/shard_map/all_to_all | solution.py:242
  79.0 4.4 %collective-permute-start.6 = (f32[544,128]{1,0:T(8,128)S(1)}, f32[544,128]{1,0:T(8,128)S(1)}, u32[]{:S(2)}, u32[]{:S(2)}) collective-permute-start(f32[544,128]{1,0:T(8,128)S(1)} %bitcast.8), channel_id=1, source_target_pairs={{0,1},{1,0},{2,3},{3,2},{4,5},{5,4},{6,7},{7,6},{8,9},{9,8},{10,11... | collective-permute-start | bytes 835592 | tf_op jit(solution)/shard_map/ppermute | solution.py:277
  83.4 1.0 collective-permute-done.6.other_ref
  84.4 12.3 %shard_map.19.inv_ref = f32[512,512]{1,0:T(8,128)S(1)} custom-call(s32[1]{0:T(128)} %bitcast.1.core_ref, f32[544,128]{1,0:T(8,128)S(1)} %bitcast.9, f32[544,128]{1,0:T(8,128)S(1)} %collective-permute-done.6.other_ref), custom_call_target="tpu_custom_call" | custom-call | tf_op jit(solution)/shard_map/pallas_call | solution.py:107
  96.7 1.4 %shard_map.20.basis_ref = f32[128,512]{1,0:T(8,128)S(1)} custom-call(s32[1]{0:T(128)} %bitcast.index_ref, f32[128,256]{1,0:T(8,128)S(1)} %add.20.mine_ref, f32[128,256]{1,0:T(8,128)S(1)} %collective-permute-done.5.other_ref, f32[512,512]{1,0:T(8,128)S(1)} %shard_map.19.inv_ref), custom_call_target="tpu_custom_call" | custom-call | tf_op jit(solution)/shard_map/pallas_call | solution.py:107
  98.1 0.0 all-to-all-done.2.gram_ref
  98.1 1.3 %shard_map.21 = f32[128,256]{1,0:T(8,128)} custom-call(s32[1]{0:T(128)} %bitcast.index_ref, f32[128,512]{1,0:T(8,128)S(1)} %shard_map.20.basis_ref, f32[32,32,128]{2,1,0:T(8,128)S(1)} %all-to-all-done.2.gram_ref, f32[128,256]{1,0:T(8,128)S(1)} %copy-done), custom_call_target="tpu_custom_call" | custom-call | tf_op jit(solution)/shard_map/pallas_call | solution.py:107
  (1 shorter events, 0.0 us)
Async XLA Ops:
  0.0 2.7 %collective-permute-start.3 = (f32[128,256]{1,0:T(8,128)}, f32[128,256]{1,0:T(8,128)S(1)}, u32[]{:S(2)}, u32[]{:S(2)}) collective-permute-start(f32[128,256]{1,0:T(8,128)} %own_ref.3), channel_id=1, source_target_pairs={{0,2},{1,3},{16,18},{17,19},{32,34},{33,35},{48,50},{49,51},{64,66... | collective-permute-start | bytes 393224 | tf_op jit(solution)/shard_map/ppermute | solution.py:262
  0.7 2.1 %collective-permute-start.2 = (f32[128,256]{1,0:T(8,128)}, f32[128,256]{1,0:T(8,128)S(1)}, u32[]{:S(2)}, u32[]{:S(2)}) collective-permute-start(f32[128,256]{1,0:T(8,128)} %own_ref.3), channel_id=1, source_target_pairs={{0,6},{1,7},{16,22},{17,23},{32,38},{33,39},{48,54},{49,55},{64,70... | collective-permute-start | bytes 393224 | tf_op jit(solution)/shard_map/ppermute | solution.py:262
  1.3 1.4 %collective-permute-start.1 = (f32[128,256]{1,0:T(8,128)}, f32[128,256]{1,0:T(8,128)S(1)}, u32[]{:S(2)}, u32[]{:S(2)}) collective-permute-start(f32[128,256]{1,0:T(8,128)} %own_ref.3), channel_id=1, source_target_pairs={{0,14},{1,15},{16,30},{17,31},{32,46},{33,47},{48,62},{49,63},{64,... | collective-permute-start | bytes 393224 | tf_op jit(solution)/shard_map/ppermute | solution.py:262
  2.0 0.7 collective-permute-start
  2.8 17.7 %copy-start = (f32[128,256]{1,0:T(8,128)S(1)}, f32[128,256]{1,0:T(8,128)}, u32[]{:S(2)}) copy-start(f32[128,256]{1,0:T(8,128)} %own_ref.3) | copy-start | bytes 393220
  2.8 12.1 %collective-permute-start.4 = (f32[128,256]{1,0:T(8,128)S(1)}, f32[128,256]{1,0:T(8,128)S(1)}, u32[]{:S(2)}, u32[]{:S(2)}) collective-permute-start(f32[128,256]{1,0:T(8,128)S(1)} %add_select_fusion), channel_id=1, source_target_pairs={{2,4},{3,5},{6,8},{7,9},{14,12},{15,13},{18,20},{19,21},{22,24},{2... | collective-permute-start | bytes 393224 | tf_op jit(solution)/shard_map/ppermute | solution.py:264
  15.0 5.5 %collective-permute-start.5 = (f32[128,256]{1,0:T(8,128)S(1)}, f32[128,256]{1,0:T(8,128)S(1)}, u32[]{:S(2)}, u32[]{:S(2)}) collective-permute-start(f32[128,256]{1,0:T(8,128)S(1)} %add.20.mine_ref), channel_id=1, source_target_pairs={{0,1},{1,0},{2,3},{3,2},{4,5},{5,4},{6,7},{7,6},{8,9},{9,8},{10,11... | collective-permute-start | bytes 393224 | tf_op jit(solution)/shard_map/ppermute | solution.py:265
  71.9 26.2 %all-to-all-start.2 = ((f32[32,32,128]{2,1,0:T(8,128)}), f32[32,32,128]{2,1,0:T(8,128)S(1)}, u32[]{:S(2)}, u32[]{:S(2)}) async-start(f32[32,32,128]{2,1,0:T(8,128)} %get-tuple-element.12), calls=%async_computation.2 | async-start | bytes 1048576 | tf_op jit(solution)/shard_map/all_to_all | solution.py:242
  79.0 5.4 %collective-permute-start.6 = (f32[544,128]{1,0:T(8,128)S(1)}, f32[544,128]{1,0:T(8,128)S(1)}, u32[]{:S(2)}, u32[]{:S(2)}) collective-permute-start(f32[544,128]{1,0:T(8,128)S(1)} %bitcast.8), channel_id=1, source_target_pairs={{0,1},{1,0},{2,3},{3,2},{4,5},{5,4},{6,7},{7,6},{8,9},{9,8},{10,11... | collective-permute-start | bytes 835592 | tf_op jit(solution)/shard_map/ppermute | solution.py:277

commit v7 on v6

--- a/solution.py
+++ b/solution.py
@@ -175,10 +175,9 @@
     return [first, second, *rest]
 
 
-def inverse_kernel(core_ref, mine_ref, other_ref, inv_ref, work_ref):
-    n = inv_ref.shape[0]
+def inverse_kernel(core_ref, mine_ref, other_ref, work_ref):
+    n = work_ref.shape[0]
     blocks = n // LANE
-    work_ref[...] = jnp.zeros_like(work_ref)
     mine, other = unfolded(mine_ref), unfolded(other_ref)
     for half in range(2):
         for at, place in enumerate(HALVES[half]):
@@ -202,11 +201,9 @@
                 if (i, j) != (k + 1, k + 1):
                     change = dot(up, work_ref[span(k), span(j)], 0, 0)
                     work_ref[span(i), span(j)] = work_ref[span(i), span(j)] - change
-    for i in range(blocks):
+    for i in range(blocks - 1):
         split = LANE * (i + 1)
-        inv_ref[span(i), :split] = work_ref[span(i), :split]
-        if split < n:
-            inv_ref[span(i), split:] = jnp.zeros((LANE, n - split), jnp.float32)
+        work_ref[span(i), split:] = jnp.zeros((LANE, n - split), jnp.float32)
 
 
 def basis_kernel(index_ref, mine_ref, other_ref, inv_ref, basis_ref):
@@ -259,7 +256,7 @@
     core, chip = index % 2, index // 2
     pairs = [(i, i ^ 1) for i in range(groups)]
 
-    given = [lax.ppermute(own, "orb", steps([(0, target)])) for target in (5, 7, 3, 1)]
+    given = [lax.ppermute(own, "orb", steps([(0, target)])) for target in (5, 3, 7, 1)]
     first = jnp.where(chip == 0, own, (given[0] + given[1]) + (given[2] + given[3]))
     mine = first + lax.ppermute(first, "orb", steps([(1, 2), (3, 4), (7, 6)]))
     other = lax.ppermute(mine, "orb", pairs)
@@ -275,10 +272,7 @@
     tiles, gram = lax.optimization_barrier((in_lines(tiles, "row"), gram))
     gram = swapped(gram, "row")
     others = lax.ppermute(tiles, "orb", pairs)
-    inverse = call(
-        inverse_kernel, [(2 * width, 2 * width)], core, tiles, others,
-        scratch=[(2 * width, 2 * width)],
-    )[0]
+    inverse = call(inverse_kernel, [(2 * width, 2 * width)], core, tiles, others)[0]
     basis = call(basis_kernel, [(rows, 2 * width)], index, mine, other, inverse)[0]
     return call(finish_kernel, [own.shape], index, basis, gram, own, near=(False,))[0]
 

time: 99.8 us -> 98.9 us (level)
  the two profiles are of different devices: /device:TPU:51 before, /device:TPU:35 now
where the time goes in v7:
time: 98.9 us; the launch traced here: 98.5 us
  blocking collectives  49.6 us (50%)
  starting transfers between devices  20 us (20%)
  Pallas kernels  16.8 us (17%)
  waiting for transfers between devices  11.8 us (12%)
    all_to_all x2, blocking collectives, swapped(): return lax.all_to_all(pieces, axis, 0, 0, tiled=True)  49.6 us
    pallas_call x5, Pallas kernels, call(): pl.pallas_call(kernel, out_shape=[kind(shape, jnp.float32) for kind, shap...  16.8 us
    ppermute x1, waiting for transfers between devices, on_device(): mine = first + lax.ppermute(first, 'orb', steps([(1, 2), (3, 4), (7, 6)]))  9.87 us
    all_to_all x1, starting transfers between devices, swapped(): return lax.all_to_all(pieces, axis, 0, 0, tiled=True)  7.12 us
    ppermute x1, starting transfers between devices, on_device(): other = lax.ppermute(mine, 'orb', pairs)  4.41 us
    ppermute x1, starting transfers between devices, on_device(): others = lax.ppermute(tiles, 'orb', pairs)  4.38 us
    ppermute x4, starting transfers between devices, on_device(): lax.ppermute(own, 'orb', steps([(0, target)]))  2.66 us
  transfers between devices with their start and end apart: 8, of which 3 were waited for; matrix products, arithmetic and copies ran while one was open for 0% of the time, Pallas kernels for 14%

profile of v7, /device:TPU:35, one launch (start us, length us, event | category | flops | bytes accessed | tf_op | source)
XLA Modules:
  0.0 98.5 jit_solution(9686564772676989120)
XLA Ops:
  0.0 0.7 collective-permute-start.3
  0.7 0.7 collective-permute-start.2
  1.3 0.7 collective-permute-start.1
  2.0 0.7 collective-permute-start
  2.7 0.0 collective-permute-done.3
  2.7 0.0 collective-permute-done.2
  2.7 0.0 collective-permute-done.1
  2.7 0.0 collective-permute-done
  2.8 0.1 add_select_fusion
  2.8 0.0 copy-start
  2.8 1.4 %collective-permute-start.4 = (f32[128,256]{1,0:T(8,128)S(1)}, f32[128,256]{1,0:T(8,128)S(1)}, u32[]{:S(2)}, u32[]{:S(2)}) collective-permute-start(f32[128,256]{1,0:T(8,128)S(1)} %add_select_fusion), channel_id=1, source_target_pairs={{2,4},{3,5},{6,8},{7,9},{14,12},{15,13},{18,20},{19,21},{22,24},{2... | collective-permute-start | bytes 393224 | tf_op jit(solution)/shard_map/ppermute | solution.py:261
  4.3 9.9 %collective-permute-done.4 = f32[128,256]{1,0:T(8,128)S(1)} collective-permute-done((f32[128,256]{1,0:T(8,128)S(1)}, f32[128,256]{1,0:T(8,128)S(1)}, u32[]{:S(2)}, u32[]{:S(2)}) %collective-permute-start.4) | collective-permute-done | bytes 131104 | tf_op jit(solution)/shard_map/ppermute | solution.py:261
  14.1 4.4 %collective-permute-start.5 = (f32[128,256]{1,0:T(8,128)S(1)}, f32[128,256]{1,0:T(8,128)S(1)}, u32[]{:S(2)}, u32[]{:S(2)}) collective-permute-start(f32[128,256]{1,0:T(8,128)S(1)} %add.20.mine_ref), channel_id=1, source_target_pairs={{0,1},{1,0},{2,3},{3,2},{4,5},{5,4},{6,7},{7,6},{8,9},{9,8},{10,11... | collective-permute-start | bytes 393224 | tf_op jit(solution)/shard_map/ppermute | solution.py:262
  18.6 1.0 collective-permute-done.5.other_ref
  19.5 0.0 copy-done
  19.5 1.0 shard_map.17
  20.5 31.6 %all_to_all.15 = f32[32,1,6272]{2,1,0:T(1,128)S(1)} all-to-all(f32[32,1,6272]{2,1,0:T(1,128)S(1)} %bitcast.7), channel_id=1, replica_groups=mesh['row'=32,'orb'=16] {'row'}, dimensions={0} | all-to-all | bytes 1605632 | tf_op jit(solution)/shard_map/all_to_all | solution.py:239
  52.1 0.9 shard_map.18
  53.0 18.0 %all_to_all.16 = f32[32,1,2176]{2,1,0:T(1,128)S(1)} all-to-all(f32[32,1,2176]{2,1,0:T(1,128)S(1)} %bitcast.10), channel_id=1, replica_groups=mesh['row'=32,'orb'=16] {'row'}, dimensions={0} | all-to-all | bytes 557056 | tf_op jit(solution)/shard_map/all_to_all | solution.py:239
  70.9 7.1 %all-to-all-start.2 = ((f32[32,32,128]{2,1,0:T(8,128)}), f32[32,32,128]{2,1,0:T(8,128)S(1)}, u32[]{:S(2)}, u32[]{:S(2)}) async-start(f32[32,32,128]{2,1,0:T(8,128)} %get-tuple-element.12), calls=%async_computation.2 | async-start | bytes 1048576 | tf_op jit(solution)/shard_map/all_to_all | solution.py:239
  78.1 4.4 %collective-permute-start.6 = (f32[544,128]{1,0:T(8,128)S(1)}, f32[544,128]{1,0:T(8,128)S(1)}, u32[]{:S(2)}, u32[]{:S(2)}) collective-permute-start(f32[544,128]{1,0:T(8,128)S(1)} %bitcast.8), channel_id=1, source_target_pairs={{0,1},{1,0},{2,3},{3,2},{4,5},{5,4},{6,7},{7,6},{8,9},{9,8},{10,11... | collective-permute-start | bytes 835592 | tf_op jit(solution)/shard_map/ppermute | solution.py:274
  82.5 1.0 collective-permute-done.6.other_ref
  83.4 12.3 %shard_map.19.inv_ref = f32[512,512]{1,0:T(8,128)S(1)} custom-call(s32[1]{0:T(128)} %bitcast.1.core_ref, f32[544,128]{1,0:T(8,128)S(1)} %bitcast.9, f32[544,128]{1,0:T(8,128)S(1)} %collective-permute-done.6.other_ref), custom_call_target="tpu_custom_call" | custom-call | tf_op jit(solution)/shard_map/pallas_call | solution.py:107
  95.7 1.4 %shard_map.20.basis_ref = f32[128,512]{1,0:T(8,128)S(1)} custom-call(s32[1]{0:T(128)} %bitcast.index_ref, f32[128,256]{1,0:T(8,128)S(1)} %add.20.mine_ref, f32[128,256]{1,0:T(8,128)S(1)} %collective-permute-done.5.other_ref, f32[512,512]{1,0:T(8,128)S(1)} %shard_map.19.inv_ref), custom_call_target="tpu_custom_call" | custom-call | tf_op jit(solution)/shard_map/pallas_call | solution.py:107
  97.2 0.0 all-to-all-done.2.gram_ref
  97.2 1.3 %shard_map.21 = f32[128,256]{1,0:T(8,128)} custom-call(s32[1]{0:T(128)} %bitcast.index_ref, f32[128,512]{1,0:T(8,128)S(1)} %shard_map.20.basis_ref, f32[32,32,128]{2,1,0:T(8,128)S(1)} %all-to-all-done.2.gram_ref, f32[128,256]{1,0:T(8,128)S(1)} %copy-done), custom_call_target="tpu_custom_call" | custom-call | tf_op jit(solution)/shard_map/pallas_call | solution.py:107
  (1 shorter events, 0.0 us)
Async XLA Ops:
  0.0 2.7 %collective-permute-start.3 = (f32[128,256]{1,0:T(8,128)}, f32[128,256]{1,0:T(8,128)S(1)}, u32[]{:S(2)}, u32[]{:S(2)}) collective-permute-start(f32[128,256]{1,0:T(8,128)} %own_ref.3), channel_id=1, source_target_pairs={{0,2},{1,3},{16,18},{17,19},{32,34},{33,35},{48,50},{49,51},{64,66... | collective-permute-start | bytes 393224 | tf_op jit(solution)/shard_map/ppermute | solution.py:259
  0.7 2.1 %collective-permute-start.2 = (f32[128,256]{1,0:T(8,128)}, f32[128,256]{1,0:T(8,128)S(1)}, u32[]{:S(2)}, u32[]{:S(2)}) collective-permute-start(f32[128,256]{1,0:T(8,128)} %own_ref.3), channel_id=1, source_target_pairs={{0,14},{1,15},{16,30},{17,31},{32,46},{33,47},{48,62},{49,63},{64,... | collective-permute-start | bytes 393224 | tf_op jit(solution)/shard_map/ppermute | solution.py:259
  1.3 1.4 %collective-permute-start.1 = (f32[128,256]{1,0:T(8,128)}, f32[128,256]{1,0:T(8,128)S(1)}, u32[]{:S(2)}, u32[]{:S(2)}) collective-permute-start(f32[128,256]{1,0:T(8,128)} %own_ref.3), channel_id=1, source_target_pairs={{0,6},{1,7},{16,22},{17,23},{32,38},{33,39},{48,54},{49,55},{64,70... | collective-permute-start | bytes 393224 | tf_op jit(solution)/shard_map/ppermute | solution.py:259
  2.0 0.7 collective-permute-start
  2.8 16.7 %copy-start = (f32[128,256]{1,0:T(8,128)S(1)}, f32[128,256]{1,0:T(8,128)}, u32[]{:S(2)}) copy-start(f32[128,256]{1,0:T(8,128)} %own_ref.3) | copy-start | bytes 393220
  2.8 11.3 %collective-permute-start.4 = (f32[128,256]{1,0:T(8,128)S(1)}, f32[128,256]{1,0:T(8,128)S(1)}, u32[]{:S(2)}, u32[]{:S(2)}) collective-permute-start(f32[128,256]{1,0:T(8,128)S(1)} %add_select_fusion), channel_id=1, source_target_pairs={{2,4},{3,5},{6,8},{7,9},{14,12},{15,13},{18,20},{19,21},{22,24},{2... | collective-permute-start | bytes 393224 | tf_op jit(solution)/shard_map/ppermute | solution.py:261
  14.1 5.4 %collective-permute-start.5 = (f32[128,256]{1,0:T(8,128)S(1)}, f32[128,256]{1,0:T(8,128)S(1)}, u32[]{:S(2)}, u32[]{:S(2)}) collective-permute-start(f32[128,256]{1,0:T(8,128)S(1)} %add.20.mine_ref), channel_id=1, source_target_pairs={{0,1},{1,0},{2,3},{3,2},{4,5},{5,4},{6,7},{7,6},{8,9},{9,8},{10,11... | collective-permute-start | bytes 393224 | tf_op jit(solution)/shard_map/ppermute | solution.py:262
  70.9 26.2 %all-to-all-start.2 = ((f32[32,32,128]{2,1,0:T(8,128)}), f32[32,32,128]{2,1,0:T(8,128)S(1)}, u32[]{:S(2)}, u32[]{:S(2)}) async-start(f32[32,32,128]{2,1,0:T(8,128)} %get-tuple-element.12), calls=%async_computation.2 | async-start | bytes 1048576 | tf_op jit(solution)/shard_map/all_to_all | solution.py:239
  78.1 5.4 %collective-permute-start.6 = (f32[544,128]{1,0:T(8,128)S(1)}, f32[544,128]{1,0:T(8,128)S(1)}, u32[]{:S(2)}, u32[]{:S(2)}) collective-permute-start(f32[544,128]{1,0:T(8,128)S(1)} %bitcast.8), channel_id=1, source_target_pairs={{0,1},{1,0},{2,3},{3,2},{4,5},{5,4},{6,7},{7,6},{8,9},{9,8},{10,11... | collective-permute-start | bytes 835592 | tf_op jit(solution)/shard_map/ppermute | solution.py:274

commit v8 on v7

--- a/solution.py
+++ b/solution.py
@@ -230,9 +230,8 @@
 
     @pl.when(index_ref[0] > 1)
     def _():
-        for h in range(2):
-            gram = gram_ref[:, span(h, BASIS // 2), :].reshape(pieces * BASIS // 2, LANE)
-            out_ref[:, span(h)] = own_ref[:, span(h)] - dot(basis_ref[...], gram)
+        halves = [gram_ref[:, span(h, BASIS // 2), :].reshape(pieces * BASIS // 2, LANE) for h in range(2)]
+        out_ref[...] = own_ref[...] - dot(basis_ref[...], jnp.concatenate(halves, axis=1))
 
 
 def swapped(pieces, axis):

time: 98.9 us -> 98.7 us (level)
  no operation moved by 1% of the time
where the time goes in v8:
time: 98.7 us; the launch traced here: 98.3 us
  blocking collectives  49.6 us (50%)
  starting transfers between devices  20 us (20%)
  Pallas kernels  16.7 us (17%)
  waiting for transfers between devices  11.8 us (12%)
    all_to_all x2, blocking collectives, swapped(): return lax.all_to_all(pieces, axis, 0, 0, tiled=True)  49.6 us
    pallas_call x5, Pallas kernels, call(): pl.pallas_call(kernel, out_shape=[kind(shape, jnp.float32) for kind, shap...  16.7 us
    ppermute x1, waiting for transfers between devices, on_device(): mine = first + lax.ppermute(first, 'orb', steps([(1, 2), (3, 4), (7, 6)]))  9.87 us
    all_to_all x1, starting transfers between devices, swapped(): return lax.all_to_all(pieces, axis, 0, 0, tiled=True)  7.12 us
    ppermute x1, starting transfers between devices, on_device(): other = lax.ppermute(mine, 'orb', pairs)  4.41 us
    ppermute x1, starting transfers between devices, on_device(): others = lax.ppermute(tiles, 'orb', pairs)  4.38 us
    ppermute x4, starting transfers between devices, on_device(): lax.ppermute(own, 'orb', steps([(0, target)]))  2.66 us
  transfers between devices with their start and end apart: 8, of which 3 were waited for; matrix products, arithmetic and copies ran while one was open for 0% of the time, Pallas kernels for 14%

profile of v8, /device:TPU:35, one launch (start us, length us, event | category | flops | bytes accessed | tf_op | source)
XLA Modules:
  0.0 98.3 jit_solution(296932525459942054)
XLA Ops:
  0.0 0.7 collective-permute-start.3
  0.7 0.7 collective-permute-start.2
  1.3 0.7 collective-permute-start.1
  2.0 0.7 collective-permute-start
  2.7 0.0 collective-permute-done.3
  2.7 0.0 collective-permute-done.2
  2.7 0.0 collective-permute-done.1
  2.7 0.0 collective-permute-done
  2.8 0.1 add_select_fusion
  2.8 0.0 copy-start
  2.8 1.4 %collective-permute-start.4 = (f32[128,256]{1,0:T(8,128)S(1)}, f32[128,256]{1,0:T(8,128)S(1)}, u32[]{:S(2)}, u32[]{:S(2)}) collective-permute-start(f32[128,256]{1,0:T(8,128)S(1)} %add_select_fusion), channel_id=1, source_target_pairs={{2,4},{3,5},{6,8},{7,9},{14,12},{15,13},{18,20},{19,21},{22,24},{2... | collective-permute-start | bytes 393224 | tf_op jit(solution)/shard_map/ppermute | solution.py:260
  4.3 9.9 %collective-permute-done.4 = f32[128,256]{1,0:T(8,128)S(1)} collective-permute-done((f32[128,256]{1,0:T(8,128)S(1)}, f32[128,256]{1,0:T(8,128)S(1)}, u32[]{:S(2)}, u32[]{:S(2)}) %collective-permute-start.4) | collective-permute-done | bytes 131104 | tf_op jit(solution)/shard_map/ppermute | solution.py:260
  14.1 4.4 %collective-permute-start.5 = (f32[128,256]{1,0:T(8,128)S(1)}, f32[128,256]{1,0:T(8,128)S(1)}, u32[]{:S(2)}, u32[]{:S(2)}) collective-permute-start(f32[128,256]{1,0:T(8,128)S(1)} %add.20.mine_ref), channel_id=1, source_target_pairs={{0,1},{1,0},{2,3},{3,2},{4,5},{5,4},{6,7},{7,6},{8,9},{9,8},{10,11... | collective-permute-start | bytes 393224 | tf_op jit(solution)/shard_map/ppermute | solution.py:261
  18.6 1.0 collective-permute-done.5.other_ref
  19.5 0.0 copy-done
  19.5 1.0 shard_map.17
  20.5 31.6 %all_to_all.15 = f32[32,1,6272]{2,1,0:T(1,128)S(1)} all-to-all(f32[32,1,6272]{2,1,0:T(1,128)S(1)} %bitcast.7), channel_id=1, replica_groups=mesh['row'=32,'orb'=16] {'row'}, dimensions={0} | all-to-all | bytes 1605632 | tf_op jit(solution)/shard_map/all_to_all | solution.py:238
  52.1 0.9 shard_map.18
  53.0 18.0 %all_to_all.16 = f32[32,1,2176]{2,1,0:T(1,128)S(1)} all-to-all(f32[32,1,2176]{2,1,0:T(1,128)S(1)} %bitcast.10), channel_id=1, replica_groups=mesh['row'=32,'orb'=16] {'row'}, dimensions={0} | all-to-all | bytes 557056 | tf_op jit(solution)/shard_map/all_to_all | solution.py:238
  70.9 7.1 %all-to-all-start.2 = ((f32[32,32,128]{2,1,0:T(8,128)}), f32[32,32,128]{2,1,0:T(8,128)S(1)}, u32[]{:S(2)}, u32[]{:S(2)}) async-start(f32[32,32,128]{2,1,0:T(8,128)} %get-tuple-element.12), calls=%async_computation.2 | async-start | bytes 1048576 | tf_op jit(solution)/shard_map/all_to_all | solution.py:238
  78.1 4.4 %collective-permute-start.6 = (f32[544,128]{1,0:T(8,128)S(1)}, f32[544,128]{1,0:T(8,128)S(1)}, u32[]{:S(2)}, u32[]{:S(2)}) collective-permute-start(f32[544,128]{1,0:T(8,128)S(1)} %bitcast.8), channel_id=1, source_target_pairs={{0,1},{1,0},{2,3},{3,2},{4,5},{5,4},{6,7},{7,6},{8,9},{9,8},{10,11... | collective-permute-start | bytes 835592 | tf_op jit(solution)/shard_map/ppermute | solution.py:273
  82.5 1.0 collective-permute-done.6.other_ref
  83.4 12.3 %shard_map.19.inv_ref = f32[512,512]{1,0:T(8,128)S(1)} custom-call(s32[1]{0:T(128)} %bitcast.1.core_ref, f32[544,128]{1,0:T(8,128)S(1)} %bitcast.9, f32[544,128]{1,0:T(8,128)S(1)} %collective-permute-done.6.other_ref), custom_call_target="tpu_custom_call" | custom-call | tf_op jit(solution)/shard_map/pallas_call | solution.py:107
  95.7 1.4 %shard_map.20.basis_ref = f32[128,512]{1,0:T(8,128)S(1)} custom-call(s32[1]{0:T(128)} %bitcast.index_ref, f32[128,256]{1,0:T(8,128)S(1)} %add.20.mine_ref, f32[128,256]{1,0:T(8,128)S(1)} %collective-permute-done.5.other_ref, f32[512,512]{1,0:T(8,128)S(1)} %shard_map.19.inv_ref), custom_call_target="tpu_custom_call" | custom-call | tf_op jit(solution)/shard_map/pallas_call | solution.py:107
  97.2 0.0 all-to-all-done.2.gram_ref
  97.2 1.1 %shard_map.21 = f32[128,256]{1,0:T(8,128)} custom-call(s32[1]{0:T(128)} %bitcast.index_ref, f32[128,512]{1,0:T(8,128)S(1)} %shard_map.20.basis_ref, f32[32,32,128]{2,1,0:T(8,128)S(1)} %all-to-all-done.2.gram_ref, f32[128,256]{1,0:T(8,128)S(1)} %copy-done), custom_call_target="tpu_custom_call" | custom-call | tf_op jit(solution)/shard_map/pallas_call | solution.py:107
  (1 shorter events, 0.0 us)
Async XLA Ops:
  0.0 2.7 %collective-permute-start.3 = (f32[128,256]{1,0:T(8,128)}, f32[128,256]{1,0:T(8,128)S(1)}, u32[]{:S(2)}, u32[]{:S(2)}) collective-permute-start(f32[128,256]{1,0:T(8,128)} %own_ref.3), channel_id=1, source_target_pairs={{0,2},{1,3},{16,18},{17,19},{32,34},{33,35},{48,50},{49,51},{64,66... | collective-permute-start | bytes 393224 | tf_op jit(solution)/shard_map/ppermute | solution.py:258
  0.7 2.1 %collective-permute-start.2 = (f32[128,256]{1,0:T(8,128)}, f32[128,256]{1,0:T(8,128)S(1)}, u32[]{:S(2)}, u32[]{:S(2)}) collective-permute-start(f32[128,256]{1,0:T(8,128)} %own_ref.3), channel_id=1, source_target_pairs={{0,14},{1,15},{16,30},{17,31},{32,46},{33,47},{48,62},{49,63},{64,... | collective-permute-start | bytes 393224 | tf_op jit(solution)/shard_map/ppermute | solution.py:258
  1.3 1.4 %collective-permute-start.1 = (f32[128,256]{1,0:T(8,128)}, f32[128,256]{1,0:T(8,128)S(1)}, u32[]{:S(2)}, u32[]{:S(2)}) collective-permute-start(f32[128,256]{1,0:T(8,128)} %own_ref.3), channel_id=1, source_target_pairs={{0,6},{1,7},{16,22},{17,23},{32,38},{33,39},{48,54},{49,55},{64,70... | collective-permute-start | bytes 393224 | tf_op jit(solution)/shard_map/ppermute | solution.py:258
  2.0 0.7 collective-permute-start
  2.8 16.7 %copy-start = (f32[128,256]{1,0:T(8,128)S(1)}, f32[128,256]{1,0:T(8,128)}, u32[]{:S(2)}) copy-start(f32[128,256]{1,0:T(8,128)} %own_ref.3) | copy-start | bytes 393220
  2.8 11.3 %collective-permute-start.4 = (f32[128,256]{1,0:T(8,128)S(1)}, f32[128,256]{1,0:T(8,128)S(1)}, u32[]{:S(2)}, u32[]{:S(2)}) collective-permute-start(f32[128,256]{1,0:T(8,128)S(1)} %add_select_fusion), channel_id=1, source_target_pairs={{2,4},{3,5},{6,8},{7,9},{14,12},{15,13},{18,20},{19,21},{22,24},{2... | collective-permute-start | bytes 393224 | tf_op jit(solution)/shard_map/ppermute | solution.py:260
  14.1 5.4 %collective-permute-start.5 = (f32[128,256]{1,0:T(8,128)S(1)}, f32[128,256]{1,0:T(8,128)S(1)}, u32[]{:S(2)}, u32[]{:S(2)}) collective-permute-start(f32[128,256]{1,0:T(8,128)S(1)} %add.20.mine_ref), channel_id=1, source_target_pairs={{0,1},{1,0},{2,3},{3,2},{4,5},{5,4},{6,7},{7,6},{8,9},{9,8},{10,11... | collective-permute-start | bytes 393224 | tf_op jit(solution)/shard_map/ppermute | solution.py:261
  70.9 26.2 %all-to-all-start.2 = ((f32[32,32,128]{2,1,0:T(8,128)}), f32[32,32,128]{2,1,0:T(8,128)S(1)}, u32[]{:S(2)}, u32[]{:S(2)}) async-start(f32[32,32,128]{2,1,0:T(8,128)} %get-tuple-element.12), calls=%async_computation.2 | async-start | bytes 1048576 | tf_op jit(solution)/shard_map/all_to_all | solution.py:238
  78.1 5.4 %collective-permute-start.6 = (f32[544,128]{1,0:T(8,128)S(1)}, f32[544,128]{1,0:T(8,128)S(1)}, u32[]{:S(2)}, u32[]{:S(2)}) collective-permute-start(f32[544,128]{1,0:T(8,128)S(1)} %bitcast.8), channel_id=1, source_target_pairs={{0,1},{1,0},{2,3},{3,2},{4,5},{5,4},{6,7},{7,6},{8,9},{9,8},{10,11... | collective-permute-start | bytes 835592 | tf_op jit(solution)/shard_map/ppermute | solution.py:273
